TPU v7x, 256 devices: a whole 4x4x8 slice. The times are simulated.
256 devices in a mesh: tm: 16 (over z, core), row: 16 (over x, y).
Axes of the slice: x: 4, y: 4, z: 8, core: 2. Of those that a mesh axis runs over, the one named last changes fastest.
Arguments:
- prior_ensemble: float32 [128, 128, 4096], P('tm', None, 'row'), may hold values from -6 to 6
- observation_data: float32 [128, 8192], P('tm', 'row'), may hold values from -24 to 24
- inverse_error_spread: float32 [8192], P('row'), may hold values from 0.024902152 to 0.24902152
- anomaly_inflation: float32 [128], P('tm'), may hold values from 1.1 to 1.4
- nonzero_tiles: float32 [64, 8, 128, 128], P('row'), may hold values from -0.1875 to 0.1875
- nonzero_tile_targets: int32 [64, 8], P('row'), may hold values from 0 to 31, as said below
Outputs:
- smoothed_ensemble: float32 [128, 128, 4096], P('tm', None, 'row')
- filtered_ensemble: float32 [128, 128, 4096], P('tm', None, 'row')
Inputs may be any that keep to these rules, and one draw needn't show every extreme that they name: `nonzero_tile_targets`: in each block row the 8 block columns are distinct.
All inputs are finite; a program needn't handle non-finite values. Where the computation divides by a largest or mean magnitude, that divisor is 1e-20 or more.
Results may differ from a plain program's by a relative error of at most 0.0003.
Values sent between devices are 32-bit elements; how exact they have to be, the bound alone decides.
A program may use at most 64 MiB of HBM per device.

v0:
```python
import jax
import jax.numpy as jnp
from jax import lax
from jax.sharding import PartitionSpec as P

NS_ITERS = 8


exact_product = lax.Precision.HIGHEST


def passed_along(shard, axis, by):
    length = lax.axis_size(axis)
    pairs = [(i, i + by) for i in range(length) if 0 <= i + by < length]
    return lax.ppermute(shard, axis, pairs)


def ensemble_transforms(info_matrix, info_vector, anomaly_inflation):
    ensemble_entries = info_matrix.shape[-1]
    identity = jnp.eye(ensemble_entries, dtype=jnp.float32)
    row_bound = jnp.max(jnp.sum(jnp.abs(info_matrix), axis=2), axis=1)
    scaled = info_matrix / row_bound[:, None, None]
    root_iter = scaled
    inv_iter = jnp.broadcast_to(identity, scaled.shape)
    for _ in range(NS_ITERS):
        update = 1.5 * identity - 0.5 * jnp.matmul(inv_iter, root_iter, precision=exact_product)
        root_iter = jnp.matmul(root_iter, update, precision=exact_product)
        inv_iter = jnp.matmul(update, inv_iter, precision=exact_product)
    inverse_root = inv_iter / jnp.sqrt(row_bound)[:, None, None]
    half_weights = jnp.einsum("tab,tb->ta", inverse_root, info_vector, precision=exact_product)
    mean_weights = jnp.einsum("tab,tb->ta", inverse_root, half_weights, precision=exact_product)
    spread_norm = float(ensemble_entries - 1) ** 0.5
    mixing = (
        mean_weights[:, :, None] / spread_norm + anomaly_inflation[:, None, None] * inverse_root
    )
    mixing = mixing - jnp.mean(mixing, axis=1, keepdims=True)
    return mixing + 1.0 / ensemble_entries


def local(
    prior_ensemble,
    observation_data,
    inverse_error_spread,
    anomaly_inflation,
    nonzero_tiles,
    nonzero_tile_targets,
):
    ensemble_entries = prior_ensemble.shape[1]
    block_size = nonzero_tiles.shape[2]
    local_rows = nonzero_tiles.shape[0] * block_size

    def observe_single_time(ensemble_shard):
        whole = lax.all_gather(ensemble_shard, "row", axis=1, tiled=True)
        column_count = whole.shape[1] // block_size
        picked = whole.reshape(ensemble_entries, column_count, block_size)[:, nonzero_tile_targets]
        result = jnp.einsum("mbkj,bkij->mbi", picked, nonzero_tiles, precision=exact_product)
        return result.reshape(ensemble_entries, local_rows)

    predicted_observations = lax.map(observe_single_time, prior_ensemble)
    obs_mean = jnp.mean(predicted_observations, axis=1)
    whitened = (
        (predicted_observations - obs_mean[:, None, :])
        * inverse_error_spread
        / float(ensemble_entries - 1) ** 0.5
    )
    innovation = (observation_data - obs_mean) * inverse_error_spread
    part_matrix = jnp.einsum("tmo,tno->tmn", whitened, whitened, precision=exact_product)
    part_vector = jnp.einsum("tmo,to->tm", whitened, innovation, precision=exact_product)
    info_matrix, info_vector = lax.psum((part_matrix, part_vector), "row")
    identity = jnp.eye(ensemble_entries, dtype=jnp.float32)
    info_matrix = info_matrix + identity
    ensemble_weight_factors = ensemble_transforms(info_matrix, info_vector, anomaly_inflation)
    filtered_ensemble = jnp.einsum(
        "fjn,fjt->fnt", ensemble_weight_factors, prior_ensemble, precision=exact_product
    )

    def backward(running, transform):
        product = jnp.matmul(transform, running, precision=exact_product)
        return (product, product)

    _, local_trailing_sum = lax.scan(backward, identity, ensemble_weight_factors, reverse=True)
    shard_product = local_trailing_sum[0]
    final_index = lax.axis_size("tm") - 1
    position = lax.axis_index("tm")

    def one_hop(turn_index, current):
        outgoing = jnp.matmul(shard_product, current, precision=exact_product)
        received = passed_along(outgoing, "tm", -1)
        return jnp.where(position == final_index, identity, received)

    trailing_sum_end = lax.fori_loop(0, final_index, one_hop, identity)
    suffix_product = jnp.einsum(
        "jmk,kl->jml", local_trailing_sum, trailing_sum_end, precision=exact_product
    )
    smoothed_ensemble = jnp.einsum(
        "fjn,fjt->fnt", suffix_product, prior_ensemble, precision=exact_product
    )
    return (smoothed_ensemble, filtered_ensemble)


def solution(mesh):
    placed = (
        P("tm", None, "row"),
        P("tm", "row"),
        P("row"),
        P("tm"),
        P("row", None, None, None),
        P("row", None),
    )
    return jax.shard_map(
        local,
        mesh=mesh,
        in_specs=placed,
        out_specs=(P("tm", None, "row"), P("tm", None, "row")),
        check_vma=False,
    )
```

profile of v0, /device:TPU:97, one launch (start us, length us, event | category | flops | bytes accessed | tf_op | source)
XLA Modules:
  0.0 752.3 jit_solution(10505249584035878029)
XLA Ops:
  8.0 500.9 %while.39 = (s32[]{:T(128)}, f32[8,128,512]{1,2,0:T(8,128)}, f32[8,128,256]{2,1,0:T(8,128)}, s32[4,8]{1,0:T(4,128)}, f32[4,8,128,128]{3,2,1,0:T(8,128)}, /*index=5*/s32[]{:T(128)}) while((s32[]{:T(128)}, f32[8,128,512]{1,2,0:T(8,128)}, f32[8,128,256]{2,1,0:T(8,128)}, s32[4,8]{1,0:T(4,128)}, f32[4,8,128,128]{3,2,1,0:T(8,128)}, ...), condition=%wide.region_1.2_spmd, body=%wide.region_0.1_spmd.sunk | while | flops 805307520 | bytes 20583292 | solution.py:59
  10.6 52.6 %all-gather.5.cloned.1.call-done = f32[1,128,4096]{1,2,0:T(8,128)} async-done(((f32[1,128,256]{1,2,0:T(8,128)}), f32[1,128,4096]{1,2,0:T(8,128)}) %all-gather.5.cloned.1.call-update) | async-done | bytes 2097168 | tf_op jit(solution)/shard_map/while/body/eval_jaxpr/all_gather | solution.py:53
  74.7 51.0 %all-gather.5.cloned.1.call-done = f32[1,128,4096]{1,2,0:T(8,128)} async-done(((f32[1,128,256]{1,2,0:T(8,128)}), f32[1,128,4096]{1,2,0:T(8,128)}) %all-gather.5.cloned.1.call-update) | async-done | bytes 2097168 | tf_op jit(solution)/shard_map/while/body/eval_jaxpr/all_gather | solution.py:53
  137.2 51.0 %all-gather.5.cloned.1.call-done = f32[1,128,4096]{1,2,0:T(8,128)} async-done(((f32[1,128,256]{1,2,0:T(8,128)}), f32[1,128,4096]{1,2,0:T(8,128)}) %all-gather.5.cloned.1.call-update) | async-done | bytes 2097168 | tf_op jit(solution)/shard_map/while/body/eval_jaxpr/all_gather | solution.py:53
  199.7 50.7 %all-gather.5.cloned.1.call-done = f32[1,128,4096]{1,2,0:T(8,128)} async-done(((f32[1,128,256]{1,2,0:T(8,128)}), f32[1,128,4096]{1,2,0:T(8,128)}) %all-gather.5.cloned.1.call-update) | async-done | bytes 2097168 | tf_op jit(solution)/shard_map/while/body/eval_jaxpr/all_gather | solution.py:53
  261.9 50.7 %all-gather.5.cloned.1.call-done = f32[1,128,4096]{1,2,0:T(8,128)} async-done(((f32[1,128,256]{1,2,0:T(8,128)}), f32[1,128,4096]{1,2,0:T(8,128)}) %all-gather.5.cloned.1.call-update) | async-done | bytes 2097168 | tf_op jit(solution)/shard_map/while/body/eval_jaxpr/all_gather | solution.py:53
  324.1 50.7 %all-gather.5.cloned.1.call-done = f32[1,128,4096]{1,2,0:T(8,128)} async-done(((f32[1,128,256]{1,2,0:T(8,128)}), f32[1,128,4096]{1,2,0:T(8,128)}) %all-gather.5.cloned.1.call-update) | async-done | bytes 2097168 | tf_op jit(solution)/shard_map/while/body/eval_jaxpr/all_gather | solution.py:53
  386.3 51.0 %all-gather.5.cloned.1.call-done = f32[1,128,4096]{1,2,0:T(8,128)} async-done(((f32[1,128,256]{1,2,0:T(8,128)}), f32[1,128,4096]{1,2,0:T(8,128)}) %all-gather.5.cloned.1.call-update) | async-done | bytes 2097168 | tf_op jit(solution)/shard_map/while/body/eval_jaxpr/all_gather | solution.py:53
  448.8 51.0 %all-gather.5.cloned.1.call-done = f32[1,128,4096]{1,2,0:T(8,128)} async-done(((f32[1,128,256]{1,2,0:T(8,128)}), f32[1,128,4096]{1,2,0:T(8,128)}) %all-gather.5.cloned.1.call-update) | async-done | bytes 2097168 | tf_op jit(solution)/shard_map/while/body/eval_jaxpr/all_gather | solution.py:53
  511.3 5.6 fusion.7
  518.5 31.1 %psum.15 = f32[8,128]{1,0:T(8,128)S(1)} all-reduce(f32[8,128]{1,0:T(8,128)S(1)} %bitcast.123), channel_id=1, replica_groups=mesh['tm'=16,'row'=16] {'row'}, use_global_device_ids=true, to_apply=%region_6.7 | all-reduce | flops 1024 | bytes 8192 | tf_op jit(solution)/shard_map/psum | solution.py:69
  549.6 60.8 %all-reduce.2.cloned.1.call-done = f32[8,128,128]{2,1,0:T(8,128)} async-done(((f32[8,128,128]{2,1,0:T(8,128)}), f32[8,128,128]{2,1,0:T(8,128)}) %all-reduce.2.cloned.1.call-update) | async-done | bytes 524304 | tf_op jit(solution)/shard_map/psum | solution.py:69
  634.7 107.5 %while.41 = (s32[]{:T(128)}, f32[128,128]{1,0:T(8,128)S(1)}, pred[]{:T(512)}, f32[128,128]{1,0:T(8,128)S(1)}, s32[]{:T(128)}) while((s32[]{:T(128)}, f32[128,128]{1,0:T(8,128)S(1)}, pred[]{:T(512)}, f32[128,128]{1,0:T(8,128)S(1)}, s32[]{:T(128)}) %tuple.93), condition=%wide.region_11.12_spmd.clone, body=%wide.region_10.11_spmd.clone.sunk | while | flops 25214976 | bytes 589926 | solution.py:91
  645.8 4.9 collective-permute-done
  652.9 4.9 collective-permute-done
  659.9 4.9 collective-permute-done
  666.9 4.9 collective-permute-done
  674.0 4.9 collective-permute-done
  681.0 4.9 collective-permute-done
  688.1 4.9 collective-permute-done
  695.1 4.9 collective-permute-done
  702.1 4.9 collective-permute-done
  709.2 4.9 collective-permute-done
  716.2 4.9 collective-permute-done
  (217 shorter events, 177.4 us)
Async XLA Ops:
  8.0 55.2 %all-gather.5.cloned.1.call-start = ((), (), s32[]{:S(2)}) async-start(), calls=%async_computation.1 | async-start | bytes 2228224 | tf_op jit(solution)/shard_map/while/body/eval_jaxpr/all_gather | solution.py:53
  72.2 53.5 %all-gather.5.cloned.1.call-start = ((), (), s32[]{:S(2)}) async-start(), calls=%async_computation.1 | async-start | bytes 2228224 | tf_op jit(solution)/shard_map/while/body/eval_jaxpr/all_gather | solution.py:53
  134.7 53.5 %all-gather.5.cloned.1.call-start = ((), (), s32[]{:S(2)}) async-start(), calls=%async_computation.1 | async-start | bytes 2228224 | tf_op jit(solution)/shard_map/while/body/eval_jaxpr/all_gather | solution.py:53
  197.2 53.2 %all-gather.5.cloned.1.call-start = ((), (), s32[]{:S(2)}) async-start(), calls=%async_computation.1 | async-start | bytes 2228224 | tf_op jit(solution)/shard_map/while/body/eval_jaxpr/all_gather | solution.py:53
  259.4 53.2 %all-gather.5.cloned.1.call-start = ((), (), s32[]{:S(2)}) async-start(), calls=%async_computation.1 | async-start | bytes 2228224 | tf_op jit(solution)/shard_map/while/body/eval_jaxpr/all_gather | solution.py:53
  321.6 53.2 %all-gather.5.cloned.1.call-start = ((), (), s32[]{:S(2)}) async-start(), calls=%async_computation.1 | async-start | bytes 2228224 | tf_op jit(solution)/shard_map/while/body/eval_jaxpr/all_gather | solution.py:53
  383.8 53.5 %all-gather.5.cloned.1.call-start = ((), (), s32[]{:S(2)}) async-start(), calls=%async_computation.1 | async-start | bytes 2228224 | tf_op jit(solution)/shard_map/while/body/eval_jaxpr/all_gather | solution.py:53
  446.3 53.5 %all-gather.5.cloned.1.call-start = ((), (), s32[]{:S(2)}) async-start(), calls=%async_computation.1 | async-start | bytes 2228224 | tf_op jit(solution)/shard_map/while/body/eval_jaxpr/all_gather | solution.py:53
  508.9 101.5 %all-reduce.2.cloned.1.call-start = ((), (), s32[]{:S(2)}) async-start(), calls=%async_computation | async-start | bytes 1048576 | tf_op jit(solution)/shard_map/psum | solution.py:69
  634.9 8.8 %collective-permute-start = (f32[128,128]{1,0:T(8,128)S(1)}, f32[128,128]{1,0:T(8,128)S(1)}, u32[]{:S(2)}, u32[]{:S(2)}) collective-permute-start(f32[128,128]{1,0:T(8,128)S(1)} %fusion.120), channel_id=1, source_target_pairs={{16,0},{32,16},{48,32},{64,48},{80,64},{96,80},{112,96},{128,112},... | collective-permute-start | bytes 196616 | tf_op jit(solution)/shard_map/while/body/eval_jaxpr/ppermute | solution.py:15
  643.9 6.8 collective-permute-start
  650.9 6.8 collective-permute-start
  658.0 6.8 collective-permute-start
  665.0 6.8 collective-permute-start
  672.1 6.8 collective-permute-start
  679.1 6.8 collective-permute-start
  686.1 6.8 collective-permute-start
  693.2 6.8 collective-permute-start
  700.2 6.8 collective-permute-start
  707.2 6.8 collective-permute-start
  714.3 6.8 collective-permute-start
  721.3 6.8 collective-permute-start
  728.4 6.8 collective-permute-start
  735.4 6.8 collective-permute-start
  (9 other events, 120.8 us)
Sparse Core Ops, SparseCore 0:
  12.2 50.9 all-gather.4
  76.3 49.3 all-gather.4
  138.8 49.3 all-gather.4
  201.0 49.3 all-gather.4
  263.2 49.3 all-gather.4
  325.4 49.3 all-gather.4
  387.9 49.3 all-gather.4
  450.5 49.3 all-gather.4
Sparse Core Ops, SparseCore 1:
  517.0 93.3 all-reduce.1
where the time goes:
time: 753 us; the launch traced here: 752 us
  waiting for transfers between devices  542 us (72%)
  matrix products  69.3 us (9%)
  local copies, waits for them, and re-layouts  51.2 us (7%)
  starting transfers between devices  31.4 us (4%)
  blocking collectives  31.1 us (4%)
  between operations  15.9 us (2%)
  other arithmetic  10 us (1%)
    all_gather x8, waiting for transfers between devices, observe_single_time(): whole = lax.all_gather(ensemble_shard, 'row', axis=1, tiled=True)  409 us
    ppermute x15, waiting for transfers between devices, passed_along(): return lax.ppermute(shard, axis, pairs)  72.4 us
    psum x1, waiting for transfers between devices, local(): info_matrix, info_vector = lax.psum((part_matrix, part_vector), 'row')  60.8 us
    dot_general x8, matrix products, observe_single_time(): jnp.einsum('mbkj,bkij->mbi', picked, nonzero_tiles, precision=exact_product)  34.8 us
    ppermute x15, starting transfers between devices, passed_along(): return lax.ppermute(shard, axis, pairs)  31.3 us
    psum x1, blocking collectives, local(): info_matrix, info_vector = lax.psum((part_matrix, part_vector), 'row')  31.1 us
    gather x8, local copies, waits for them, and re-layouts, observe_single_time(): whole.reshape(ensemble_entries, column_count, block_size)  15.9 us
    reshape x8, local copies, waits for them, and re-layouts, observe_single_time(): whole.reshape(ensemble_entries, column_count, block_size)  15.3 us
  transfers between devices with their start and end apart: 24, of which 24 were waited for; matrix products, arithmetic and copies ran while one was open for 1% of the time, Pallas kernels for 0%

commit v1 on v0

v1 whole, which is shorter than its diff:
```python
import functools

import jax
import jax.numpy as jnp
from jax import lax
from jax.experimental import pallas as pl
from jax.experimental.pallas import tpu as pltpu
from jax.sharding import PartitionSpec as P

MESH = pl.DeviceIdType.MESH
NS_ITERS = 8
F32, BF16 = jnp.float32, jnp.bfloat16
NT = (((1,), (1,)), ((), ()))


def halves(value):
    high = value.astype(BF16)
    low = (value - high.astype(F32)).astype(BF16)
    return high, low


def product(left, right):
    lh, ll = halves(left)
    rh, rl = halves(right)
    row = jnp.concatenate([rh, rl], axis=1)
    wide = jnp.dot(
        jnp.concatenate([lh, ll], axis=1),
        jnp.concatenate([row, row], axis=0),
        preferred_element_type=F32,
    )
    n = right.shape[1]
    return wide[:, :n] + wide[:, n:]


def assimilate(
    x_ref, tiles_ref, obs_ref, spread_ref, targets_ref, inflation_ref,
    u_ref, s_ref,
    xg, tg, obg, spg, tgg, tgs, xh, xl, acc, part, parts, vbuf, vin, rloc,
    send, recv, local_sem,
):
    tm, row = lax.axis_index("tm"), lax.axis_index("row")
    mx, my = lax.div(row, 4), lax.rem(row, 4)
    last_tm = lax.axis_size("tm") - 1
    counter = [0]

    def at(x, y):
        return (tm, lax.rem(x + 4, 4) * 4 + lax.rem(y + 4, 4))

    def remote(src, dst, device):
        i = counter[0]
        counter[0] += 1
        return pltpu.make_async_remote_copy(
            src_ref=src, dst_ref=dst, send_sem=send.at[i], recv_sem=recv.at[i],
            device_id=device, device_id_type=MESH,
        )

    barrier = pltpu.get_barrier_semaphore()
    for d in (1, 2, 3):
        for device in (at(mx + d, my), at(mx, my + d)):
            pl.semaphore_signal(barrier, inc=1, device_id=device, device_id_type=MESH)
    peers = 6
    for d in (1, 2, 4, 8):
        @pl.when(tm >= d)
        def _():
            pl.semaphore_signal(barrier, inc=1, device_id=(tm - d, row), device_id_type=MESH)

        @pl.when(tm + d <= last_tm)
        def _():
            pl.semaphore_signal(barrier, inc=1, device_id=(tm + d, row), device_id_type=MESH)

        peers = peers + jnp.where(tm >= d, 1, 0) + jnp.where(tm + d <= last_tm, 1, 0)
    pl.semaphore_wait(barrier, peers)

    core = lax.rem(tm, 2)
    other = (tm + 1 - 2 * core, row)
    sent = []

    def start(copy):
        copy.start()
        sent.append(copy)
        return copy

    own_x = x_ref.at[pl.ds(2 * mx, 2)]
    across = {}
    for d in (1, 3, 2):
        xd = lax.rem(mx + d, 4)
        across[d] = start(remote(x_ref.at[pl.ds(2 * xd, 2)], xg.at[d, 0], at(mx + d, my)))
    up, down, up2, down2 = {}, {}, {}, {}
    up[0] = start(remote(own_x, xg.at[0, 1], at(mx, my + 1)))
    down[0] = start(remote(own_x, xg.at[0, 3], at(mx, my - 1)))
    small = []
    for d in (1, 2, 3):
        xd = lax.rem(mx + d, 4)
        small.append(start(remote(obs_ref.at[pl.ds(2 * xd, 2)], obg.at[d], at(mx + d, my))))
        small.append(start(remote(spread_ref, spg.at[d], at(mx + d, my))))
        small.append(start(remote(targets_ref, tgg.at[d], at(mx + d, my))))
    first, second = 2 * core, 2 * core + 1
    right, left = {}, {}
    right[0] = start(remote(tiles_ref.at[first], tg.at[1, first], at(mx + 1, my)))
    left[0] = start(remote(tiles_ref.at[second], tg.at[3, second], at(mx - 1, my)))
    right[1] = start(remote(tiles_ref.at[second], tg.at[1, second], at(mx + 1, my)))
    left[1] = start(remote(tiles_ref.at[first], tg.at[3, first], at(mx - 1, my)))

    locals_ = [
        pltpu.make_async_copy(own_x, xg.at[0, 0], local_sem.at[0]),
        pltpu.make_async_copy(tiles_ref, tg.at[0], local_sem.at[1]),
        pltpu.make_async_copy(obs_ref.at[pl.ds(2 * mx, 2)], obg.at[0], local_sem.at[2]),
        pltpu.make_async_copy(spread_ref, spg.at[0], local_sem.at[3]),
        pltpu.make_async_copy(targets_ref, tgg.at[0], local_sem.at[4]),
    ]
    for copy in locals_:
        copy.start()

    def split_state(k, q):
        chunk = lax.rem(mx - k + 4, 4) * 4 + lax.rem(my - q + 4, 4)
        for t in (0, 1):
            for half in (0, 1):
                high, low = halves(xg[k, q, t, :, half * 128:(half + 1) * 128])
                xh[2 * chunk + half, t * 128:(t + 1) * 128, :] = high
                xl[2 * chunk + half, t * 128:(t + 1) * 128, :] = low

    for d in (1, 3, 2):
        across[d].wait_recv()
        up[d] = start(remote(xg.at[d, 0], xg.at[d, 1], at(mx, my + 1)))
        down[d] = start(remote(xg.at[d, 0], xg.at[d, 3], at(mx, my - 1)))
    for copy in locals_:
        copy.wait()
    for k in (0, 1, 3, 2):
        up[k].wait_recv()
        up2[k] = start(remote(xg.at[k, 1, 0], xg.at[k, 2, 0], at(mx, my + 1)))
        down[k].wait_recv()
        down2[k] = start(remote(xg.at[k, 3, 1], xg.at[k, 2, 1], at(mx, my - 1)))
        if k == 1:
            right[0].wait_recv()
            right2 = start(remote(tg.at[1, first], tg.at[2, first], at(mx + 1, my)))
            left[0].wait_recv()
            left2 = start(remote(tg.at[3, second], tg.at[2, second], at(mx - 1, my)))
        split_state(k, 0)
        split_state(k, 1)
        split_state(k, 3)
    passed = [
        start(remote(tg.at[1, first], tg.at[1, first], other)),
        start(remote(tg.at[3, second], tg.at[3, second], other)),
    ]
    right[1].wait_recv()
    passed.append(start(remote(tg.at[1, second], tg.at[1, second], other)))
    left[1].wait_recv()
    passed.append(start(remote(tg.at[3, first], tg.at[3, first], other)))
    for k in (0, 1, 3, 2):
        up2[k].wait_recv()
        down2[k].wait_recv()
        split_state(k, 2)
    right2.wait_recv()
    passed.append(start(remote(tg.at[2, first], tg.at[2, first], other)))
    left2.wait_recv()
    passed.append(start(remote(tg.at[2, second], tg.at[2, second], other)))
    for copy in small:
        copy.wait_recv()
    to_scalar = pltpu.make_async_copy(tgg, tgs, local_sem.at[0])
    to_scalar.start()
    to_scalar.wait()
    for copy in passed:
        copy.wait_recv()

    acc[...] = jnp.zeros_like(acc)

    def block_row(b, carry):
        k, i = lax.div(b, 4), lax.rem(b, 4)
        index = [tgs[k, i, j] for j in range(8)]
        th, tl = [], []
        for j in range(8):
            high, low = halves(tg[k, i, j])
            th.append(high)
            tl.append(low)
        th = jnp.concatenate(th, axis=1)
        tl = jnp.concatenate(tl, axis=1)
        high = jnp.concatenate([xh[j] for j in index], axis=1)
        low = jnp.concatenate([xl[j] for j in index], axis=1)
        wide = lax.dot_general(high, jnp.concatenate([th, tl], axis=0), NT, preferred_element_type=F32)
        obs = wide[:, :128] + wide[:, 128:]
        obs = obs + lax.dot_general(low, th, NT, preferred_element_type=F32)
        spread = spg[k, pl.ds(i, 1), :]
        for t in (0, 1):
            one = obs[t * 128:(t + 1) * 128, :]
            mean = jnp.sum(one, axis=0, keepdims=True) * (1.0 / 128.0)
            wh, wl = halves((one - mean) * (spread * (127.0 ** -0.5)))
            innovation = (obg[k, t, pl.ds(i, 1), :] - mean) * spread
            ih, il = halves(jnp.broadcast_to(innovation, (16, 128)))
            upper = lax.broadcasted_iota(jnp.int32, (16, 128), 0) < 8
            lines = jnp.where(upper, ih.astype(F32), il.astype(F32)).astype(BF16)
            acc[t] += lax.dot_general(
                jnp.concatenate([wh, lines], axis=0), jnp.concatenate([wh, wl], axis=0), NT,
                preferred_element_type=F32,
            )
        return carry

    lax.fori_loop(0, 16, block_row, 0)

    for t in (0, 1):
        cross = acc[t, 0:128, 128:256]
        part[t, 0:128, :] = acc[t, 0:128, 0:128] + cross + cross.T
        part[t, 128:136, :] = acc[t, 128:136, 0:128] + acc[t, 128:136, 128:256] + acc[t, 136:144, 0:128]
    sums = [start(remote(part, parts.at[d], at(mx, my + d))) for d in (1, 2, 3)]
    for copy in sums:
        copy.wait_recv()

    eye = (
        lax.broadcasted_iota(jnp.int32, (128, 128), 0) == lax.broadcasted_iota(jnp.int32, (128, 128), 1)
    ).astype(F32)
    state = []
    for t in (0, 1):
        total = part[t] + parts[1, t] + parts[2, t] + parts[3, t]
        info = total[0:128, :] + eye
        bound = jnp.max(jnp.sum(jnp.abs(info), axis=0, keepdims=True), axis=1, keepdims=True)
        m = info / bound
        state.append([m, 1.5 * eye - 0.5 * m, bound, total[128:136, :]])
    for _ in range(NS_ITERS - 1):
        for s in state:
            square = product(s[0], s[0])
            s[0] = product(s[0], 2.25 * eye - 1.5 * s[0] + 0.25 * square)
            s[1] = product(1.5 * eye - 0.5 * s[0], s[1])
    for t, (_, q, bound, vector) in enumerate(state):
        root = q / jnp.sqrt(bound)
        weights = product(product(vector, root), root)[0:1, :]
        mixing = weights * (127.0 ** -0.5) + inflation_ref[2 * mx + t] * root
        mixing = mixing - jnp.sum(mixing, axis=1, keepdims=True) * (1.0 / 128.0) + 1.0 / 128.0
        u_ref[2 * mx + t] = mixing
    mine = u_ref.at[pl.ds(2 * mx, 2)]
    shared = [start(remote(mine, mine, at(mx + d, my))) for d in (1, 2, 3)]
    for copy in shared:
        copy.wait_recv()

    u = [u_ref[t] for t in range(8)]
    p67, p45, p23, p01 = product(u[7], u[6]), product(u[5], u[4]), product(u[3], u[2]), product(u[1], u[0])
    p47 = product(p67, p45)
    p03 = product(p23, p01)
    p07 = product(p47, p03)
    running = p07
    vbuf[0] = running
    rloc[0] = p07
    rloc[4] = p47
    rloc[6] = p67
    rloc[7] = u[7]
    later = eye
    for level, d in enumerate((1, 2, 4, 8)):
        copy = remote(vbuf.at[level], vin.at[level], (tm - d, row))

        @pl.when(tm >= d)
        def _(copy=copy):
            copy.start()

        if level == 0:
            r5, r2 = product(p67, u[5]), product(p47, p23)
            rloc[5] = r5
            rloc[2] = r2
            rloc[3] = product(p47, u[3])
            rloc[1] = product(r2, u[1])

        @pl.when(tm + d <= last_tm)
        def _(copy=copy):
            copy.wait_recv()

        @pl.when(tm + d > last_tm)
        def _(level=level):
            vin[level] = eye

        got = vin[level]
        if level < 3:
            vbuf[level + 1] = product(got, vbuf[level])
        later = product(got, later)

        @pl.when(tm >= d)
        def _(copy=copy):
            copy.wait_send()

    for t in range(8):
        s_ref[t] = product(later, rloc[t])
    for copy in sent:
        copy.wait_send()


def apply(u_ref, s_ref, x_ref, smooth_ref, filter_ref):
    xh, xl = halves(x_ref[0])
    low = jnp.concatenate([xh, xl], axis=0)
    for m_ref, out_ref in ((s_ref, smooth_ref), (u_ref, filter_ref)):
        mh, ml = halves(m_ref[0])
        out_ref[0] = jnp.dot(jnp.concatenate([mh, mh], axis=1), low, preferred_element_type=F32) + jnp.dot(
            ml, xh, preferred_element_type=F32
        )


def local(prior, observations, spread, inflation, tiles, targets):
    obs = jnp.pad(observations.reshape(8, 4, 128), ((0, 0), (0, 4), (0, 0)))
    spr = jnp.pad(spread.reshape(4, 128), ((0, 4), (0, 0)))
    tgt = jnp.pad(targets, ((0, 4), (0, 120)))
    anywhere = pl.BlockSpec(memory_space=pl.ANY)
    vmem = pl.BlockSpec(memory_space=pltpu.VMEM)
    smem = pl.BlockSpec(memory_space=pltpu.SMEM)
    square = jax.ShapeDtypeStruct((8, 128, 128), F32)
    u, s = pl.pallas_call(
        assimilate,
        out_shape=(square, square),
        in_specs=[anywhere, anywhere, vmem, vmem, vmem, smem],
        out_specs=(vmem, vmem),
        scratch_shapes=[
            pltpu.VMEM((4, 4, 2, 128, 256), F32),
            pltpu.VMEM((4, 4, 8, 128, 128), F32),
            pltpu.VMEM((4, 2, 8, 128), F32),
            pltpu.VMEM((4, 8, 128), F32),
            pltpu.VMEM((4, 8, 128), jnp.int32),
            pltpu.SMEM((4, 8, 128), jnp.int32),
            pltpu.VMEM((32, 256, 128), BF16),
            pltpu.VMEM((32, 256, 128), BF16),
            pltpu.VMEM((2, 144, 256), F32),
            pltpu.VMEM((2, 136, 128), F32),
            pltpu.VMEM((4, 2, 136, 128), F32),
            pltpu.VMEM((4, 128, 128), F32),
            pltpu.VMEM((4, 128, 128), F32),
            pltpu.VMEM((8, 128, 128), F32),
            pltpu.SemaphoreType.DMA((64,)),
            pltpu.SemaphoreType.DMA((64,)),
            pltpu.SemaphoreType.DMA((5,)),
        ],
        compiler_params=pltpu.CompilerParams(
            collective_id=0, has_side_effects=True, vmem_limit_bytes=40 << 20
        ),
        name="assimilate",
    )(prior, tiles, obs, spr, tgt, inflation)
    step = lambda t: (t, 0, 0)
    whole = jax.ShapeDtypeStruct(prior.shape, F32)
    return pl.pallas_call(
        apply,
        grid=(8,),
        out_shape=(whole, whole),
        in_specs=[
            pl.BlockSpec((1, 128, 128), step),
            pl.BlockSpec((1, 128, 128), step),
            pl.BlockSpec((1, 128, 256), step),
        ],
        out_specs=(pl.BlockSpec((1, 128, 256), step), pl.BlockSpec((1, 128, 256), step)),
        name="apply",
    )(u, s, prior)


def solution(mesh):
    placed = (
        P("tm", None, "row"),
        P("tm", "row"),
        P("row"),
        P("tm"),
        P("row", None, None, None),
        P("row", None),
    )
    return jax.shard_map(
        local,
        mesh=mesh,
        in_specs=placed,
        out_specs=(P("tm", None, "row"), P("tm", None, "row")),
        check_vma=False,
    )
```

time: 753 us -> 121 us (0.16)
  the two profiles are of different devices: /device:TPU:97 before, /device:TPU:1 now
where the time goes in v1:
time: 121 us; the launch traced here: 120 us
  Pallas kernels  113 us (93%)
  local copies, waits for them, and re-layouts  7.14 us (6%)
    pallas_call x1, Pallas kernels, local(): pl.pallas_call(assimilate, out_shape=(square, square), in_specs=[anywhere...  106 us
    pallas_call x1, Pallas kernels, local(): pl.pallas_call(apply, grid=(8,), out_shape=(whole, whole), in_specs=[pl.B...  6.46 us
    unnamed x10, local copies, waits for them, and re-layouts  5.04 us

profile of v1, /device:TPU:1, one launch (start us, length us, event | category | flops | bytes accessed | tf_op | source)
XLA Modules:
  0.0 120.3 jit_solution(7466276638635235048)
XLA Ops:
  0.6 0.7 pad.13.spread_ref
  1.3 0.7 pad.14.targets_ref
  2.0 0.7 reshape.10
  2.7 0.0 copy-start
  2.8 1.2 %copy-done = f32[8,128,256]{2,1,0:T(8,128)S(1)} copy-done((f32[8,128,256]{2,1,0:T(8,128)S(1)}, f32[8,128,256]{2,1,0:T(8,128)}, u32[]{:S(2)}) %copy-start) | copy-done | bytes 1048600
  4.0 0.0 copy-start.1
  4.0 1.6 %copy-done.1 = f32[4,8,128,128]{3,2,1,0:T(8,128)S(1)} copy-done((f32[4,8,128,128]{3,2,1,0:T(8,128)S(1)}, f32[4,8,128,128]{3,2,1,0:T(8,128)}, u32[]{:S(2)}) %copy-start.1) | copy-done | bytes 2097176
  5.6 0.0 copy-start.4
  5.6 0.7 copy-done.4
  6.2 106.1 %assimilate.1 = (f32[8,128,128]{2,1,0:T(8,128)S(1)}, f32[8,128,128]{2,1,0:T(8,128)S(1)}) custom-call(f32[8,128,256]{2,1,0:T(8,128)S(1)} %copy-done, f32[4,8,128,128]{3,2,1,0:T(8,128)S(1)} %copy-done.1, f32[8,8,128]{2,1,0:T(8,128)S(1)} %pad.12.obs_ref, f32[8,128]{1,0:T(8,128)S(1)} %pad.13.spread_ref, s32[8,128]{1,0:T(8,128)S(1)} %pad.14.targets_ref, ...), custom_call_target="tpu_custom_call" | custom-call | tf_op jit(solution)/shard_map/assimilate/pallas_call | solution.py:300
  112.3 0.0 copy-start.2
  112.3 0.8 copy-done.2
  113.1 0.0 copy-start.3
  113.1 0.8 copy-done.3
  113.9 6.5 %apply.1 = (f32[8,128,256]{2,1,0:T(8,128)}, f32[8,128,256]{2,1,0:T(8,128)}) custom-call(f32[8,128,128]{2,1,0:T(8,128)} %copy-done.2, f32[8,128,128]{2,1,0:T(8,128)} %copy-done.3, f32[8,128,256]{2,1,0:T(8,128)} %x_ref.3), custom_call_target="tpu_custom_call" | custom-call | tf_op jit(solution)/shard_map/apply/pallas_call | solution.py:331
  (1 shorter events, 0.0 us)
Async XLA Ops:
  2.7 1.2 %copy-start = (f32[8,128,256]{2,1,0:T(8,128)S(1)}, f32[8,128,256]{2,1,0:T(8,128)}, u32[]{:S(2)}) copy-start(f32[8,128,256]{2,1,0:T(8,128)} %x_ref.3) | copy-start | bytes 3145732
  4.0 1.6 %copy-start.1 = (f32[4,8,128,128]{3,2,1,0:T(8,128)S(1)}, f32[4,8,128,128]{3,2,1,0:T(8,128)}, u32[]{:S(2)}) copy-start(f32[4,8,128,128]{3,2,1,0:T(8,128)} %tiles_ref.1) | copy-start | bytes 6291460
  5.6 0.7 copy-start.4
  112.3 0.8 copy-start.2
  113.1 0.8 copy-start.3

commit v2 on v1

v2 whole, which is shorter than its diff:
```python
import functools

import jax
import jax.numpy as jnp
from jax import lax
from jax.experimental import pallas as pl
from jax.experimental.pallas import tpu as pltpu
from jax.sharding import PartitionSpec as P

MESH = pl.DeviceIdType.MESH
NS_ITERS = 8
VMEM_LIMIT = 58 << 20
F32, BF16 = jnp.float32, jnp.bfloat16
NT = (((1,), (1,)), ((), ()))


def halves(value):
    high = value.astype(BF16)
    low = (value - high.astype(F32)).astype(BF16)
    return high, low


def product(left, right):
    lh, ll = halves(left)
    rh, rl = halves(right)
    row = jnp.concatenate([rh, rl], axis=1)
    wide = jnp.dot(
        jnp.concatenate([lh, ll], axis=1),
        jnp.concatenate([row, row], axis=0),
        preferred_element_type=F32,
    )
    n = right.shape[1]
    return wide[:, :n] + wide[:, n:]


PIECE = 192
SHARED = 16 * PIECE
STEPS, BLOCK_ROWS = 2, 16


def assimilate(
    x_ref, tiles_ref, obs_ref, spread_ref, targets_ref, inflation_ref,
    smooth_ref, filter_ref,
    xg, tg, xs, ts, xown, xah, xal, obg, spg, tgg, tgs, infl, acc, part, parts,
    u_ref, pbuf, vbuf, vin, rloc, yloc,
    send, recv, local_sem,
):
    tm, row = lax.axis_index("tm"), lax.axis_index("row")
    mx, my = lax.div(row, 4), lax.rem(row, 4)
    last_tm = 15
    counter = [0]

    def at(x, y):
        return (tm, lax.rem(x + 4, 4) * 4 + lax.rem(y + 4, 4))

    def along(d):
        return (lax.rem(tm + d + 16, 16), row)

    def remote(src, dst, device):
        i = counter[0]
        counter[0] += 1
        return pltpu.make_async_remote_copy(
            src_ref=src, dst_ref=dst, send_sem=send.at[i], recv_sem=recv.at[i],
            device_id=device, device_id_type=MESH,
        )

    own_x = lambda t: x_ref.at[2 * mx + t]
    own = [
        pltpu.make_async_copy(tiles_ref, tg.at[0], local_sem.at[0]),
        pltpu.make_async_copy(x_ref, xown, local_sem.at[1]),
        pltpu.make_async_copy(obs_ref, obg.at[0], local_sem.at[2]),
        pltpu.make_async_copy(spread_ref, spg.at[0], local_sem.at[3]),
        pltpu.make_async_copy(targets_ref, tgg.at[0], local_sem.at[4]),
        pltpu.make_async_copy(inflation_ref, infl, local_sem.at[5]),
        pltpu.make_async_copy(own_x(0), xg.at[0, 0, 0], local_sem.at[6]),
        pltpu.make_async_copy(own_x(1), xg.at[0, 0, 1], local_sem.at[7]),
    ]
    for copy in own:
        copy.start()

    barrier = pltpu.get_barrier_semaphore()
    near = [at(mx + d, my) for d in (1, 2, 3)] + [at(mx, my + d) for d in (1, 2, 3)]
    near += [along(d) for d in (1, -1, 2, -2, 4, -4, 8)]
    for device in near:
        pl.semaphore_signal(barrier, inc=1, device_id=device, device_id_type=MESH)
    pl.semaphore_wait(barrier, len(near))

    core = lax.rem(tm, 2)
    z = lax.div(tm, 2)
    other = (tm + 1 - 2 * core, row)
    sent = []

    def start(copy):
        copy.start()
        sent.append(copy)
        return copy

    across, up, down = {}, {}, {}

    def send_across(t):
        for d in (1, 3, 2):
            xd = lax.rem(mx + d, 4)
            across[t, d] = start(remote(x_ref.at[2 * xd + t], xg.at[d, 0, t], at(mx + d, my)))

    def send_y(t, k):
        src = own_x(t) if k == 0 else xg.at[k, 0, t]
        up[t, k] = start(remote(src, xg.at[k, 1, t], at(mx, my + 1)))
        down[t, k] = start(remote(src, xg.at[k, 3, t], at(mx, my - 1)))

    def send_y2(t):
        up[t, 4] = start(remote(xg.at[:, 1, t, 0:64], xg.at[:, 2, t, 0:64], at(mx, my + 1)))
        down[t, 4] = start(remote(xg.at[:, 3, t, 64:128], xg.at[:, 2, t, 64:128], at(mx, my - 1)))

    send_across(0)
    send_y(0, 0)
    piece = pl.ds(PIECE * tm, PIECE)
    brought = [start(remote(tiles_ref.at[piece], tg.at[d, piece], at(mx + d, my))) for d in (1, 3, 2)]
    send_across(1)
    rest = (4096 - SHARED) // 4
    first = pl.ds(SHARED + 2 * rest * core, rest)
    second = pl.ds(SHARED + 2 * rest * core + rest, rest)
    right = [start(remote(tiles_ref.at[first], tg.at[1, first], at(mx + 1, my)))]
    left = [start(remote(tiles_ref.at[second], tg.at[3, second], at(mx - 1, my)))]
    right.append(start(remote(tiles_ref.at[second], tg.at[1, second], at(mx + 1, my))))
    left.append(start(remote(tiles_ref.at[first], tg.at[3, first], at(mx - 1, my))))
    small = []
    for d in (1, 2, 3):
        small.append(start(remote(obs_ref, obg.at[d], at(mx + d, my))))
        small.append(start(remote(spread_ref, spg.at[d], at(mx + d, my))))
        small.append(start(remote(targets_ref, tgg.at[d], at(mx + d, my))))

    passed = []

    def unit(step, low=0, size=PIECE):
        at_z = lax.rem(z + step + 8, 8)
        return tg.at[pl.ds(1, 3), pl.ds(PIECE * (2 * at_z + core) + low, size)]

    def send_z(step):
        if step < 4:
            ahead = start(remote(unit(1 - step), unit(1 - step), along(2)))
            behind = start(remote(unit(step - 1), unit(step - 1), along(-2)))
        else:
            half = PIECE // 2
            ahead = start(remote(unit(-3, 0, half), unit(-3, 0, half), along(2)))
            behind = start(remote(unit(3, half, half), unit(3, half, half), along(-2)))
        return ahead, behind

    def pass_on(ref):
        passed.append(start(remote(ref, ref, other)))

    def split_state(t, k, q):
        chunk = lax.rem(mx - k + 4, 4) * 4 + lax.rem(my - q + 4, 4)
        for half in (0, 1):
            high, low = halves(xg[k, q, t, :, half * 128:(half + 1) * 128])
            xs[t, 2 * chunk + half, 0:128, :] = high
            xs[t, 2 * chunk + half, 128:256, :] = low

    def split_tiles(k):
        @pl.loop(0, 32)
        def _(n):
            high, low = halves(tg[k, pl.ds(pl.multiple_of(n * 128, 128), 128), :])
            ts[k * 32 + n, 0:128, :] = high
            ts[k * 32 + n, 128:256, :] = low

    def observe(t, k):
        for i in range(4):
            index = [tgs[k, i, j] for j in range(8)]
            state = jnp.concatenate([xs[t, j] for j in index], axis=1)
            block = jnp.concatenate([ts[(k * 4 + i) * 8 + j] for j in range(8)], axis=1)
            wide = lax.dot_general(state, block, NT, preferred_element_type=F32)
            one = (wide[0:128, 0:128] + wide[0:128, 128:256]) + (wide[128:256, 0:128] + wide[128:256, 128:256])
            spread = spg[k, i:i + 1, :]
            mean = jnp.sum(one, axis=0, keepdims=True) * (1.0 / 128.0)
            wh, wl = halves((one - mean) * (spread * (127.0 ** -0.5)))
            seen = jnp.where(chosen[t], obg[k, :, i * 128:(i + 1) * 128], 0.0)
            innovation = (jnp.sum(seen, axis=0, keepdims=True) - mean) * spread
            ih, il = halves(jnp.broadcast_to(innovation, (16, 128)))
            upper = lax.broadcasted_iota(jnp.int32, (16, 128), 0) < 8
            lines = jnp.where(upper, ih.astype(F32), il.astype(F32)).astype(BF16)
            acc[t] += lax.dot_general(
                jnp.concatenate([wh, lines], axis=0), jnp.concatenate([wh, wl], axis=0), NT,
                preferred_element_type=F32,
            )

    def reduce(t):
        cross = acc[t, 0:128, 128:256]
        part[t, 0:128, :] = acc[t, 0:128, 0:128] + cross + cross.T
        part[t, 128:136, :] = acc[t, 128:136, 0:128] + acc[t, 128:136, 128:256] + acc[t, 136:144, 0:128]
        return [start(remote(part.at[t], parts.at[d, t], at(mx, my + d))) for d in (1, 3, 2)]

    acc[...] = jnp.zeros_like(acc)
    chosen = [lax.broadcasted_iota(jnp.int32, (8, 128), 0) == 2 * mx + t for t in (0, 1)]
    for d in (1, 3, 2):
        across[0, d].wait_recv()
        send_y(0, d)
    for copy in brought:
        copy.wait_recv()
    steps = [send_z(1)]
    pass_on(unit(0))
    send_y(1, 0)
    for copy in own:
        copy.wait()
    split_tiles(0)
    for copy in steps[0]:
        copy.wait_recv()
    steps.append(send_z(2))
    pass_on(unit(-1))
    pass_on(unit(1))
    for k in (0, 1, 3, 2):
        up[0, k].wait_recv()
        down[0, k].wait_recv()
    send_y2(0)
    for d in (1, 3, 2):
        across[1, d].wait_recv()
        send_y(1, d)
    right[0].wait_recv()
    right2 = start(remote(tg.at[1, first], tg.at[2, first], at(mx + 1, my)))
    left[0].wait_recv()
    left2 = start(remote(tg.at[3, second], tg.at[2, second], at(mx - 1, my)))
    right[1].wait_recv()
    left[1].wait_recv()
    pass_on(tg.at[1, pl.ds(SHARED + 2 * rest * core, 2 * rest)])
    pass_on(tg.at[3, pl.ds(SHARED + 2 * rest * core, 2 * rest)])
    for copy in small:
        copy.wait_recv()
    to_scalar = pltpu.make_async_copy(tgg, tgs, local_sem.at[0])
    to_scalar.start()
    for k in range(4):
        split_state(0, k, 0)
        split_state(0, k, 1)
        split_state(0, k, 3)
    for copy in steps[1]:
        copy.wait_recv()
    steps.append(send_z(3))
    pass_on(unit(-2))
    pass_on(unit(2))
    for k in range(4):
        split_state(1, k, 0)
    for t in range(8):
        xah[t], xal[t] = halves(xown[t])
    up[0, 4].wait_recv()
    down[0, 4].wait_recv()
    for k in range(4):
        split_state(0, k, 2)
    to_scalar.wait()
    for copy in steps[2]:
        copy.wait_recv()
    steps.append(send_z(4))
    pass_on(unit(-3))
    pass_on(unit(3))
    observe(0, 0)
    right2.wait_recv()
    left2.wait_recv()
    pass_on(tg.at[2, pl.ds(SHARED + 2 * rest * core, 2 * rest)])
    for k in (0, 1, 3, 2):
        up[1, k].wait_recv()
        down[1, k].wait_recv()
    send_y2(1)
    for copy in steps[3]:
        copy.wait_recv()
    pass_on(unit(4))
    for k in range(4):
        split_state(1, k, 1)
        split_state(1, k, 3)
    for copy in passed:
        copy.wait_recv()
    for k in (1, 2, 3):
        split_tiles(k)
        observe(0, k)
    sums = reduce(0)
    up[1, 4].wait_recv()
    down[1, 4].wait_recv()
    for k in range(4):
        split_state(1, k, 2)
    for k in range(4):
        observe(1, k)
    sums += reduce(1)
    for copy in sums:
        copy.wait_recv()

    eye = (
        lax.broadcasted_iota(jnp.int32, (128, 128), 0) == lax.broadcasted_iota(jnp.int32, (128, 128), 1)
    ).astype(F32)
    state = []
    for t in (0, 1):
        total = part[t] + parts[1, t] + parts[2, t] + parts[3, t]
        info = total[0:128, :] + eye
        bound = jnp.max(jnp.sum(jnp.abs(info), axis=0, keepdims=True), axis=1, keepdims=True)
        m = info / bound
        state.append([m, 1.5 * eye - 0.5 * m, bound, total[128:136, :]])
    for _ in range(NS_ITERS - 1):
        for s in state:
            square = product(s[0], s[0])
            s[0] = product(s[0], 2.25 * eye - 1.5 * s[0] + 0.25 * square)
            s[1] = product(1.5 * eye - 0.5 * s[0], s[1])
    for t, (_, q, bound, vector) in enumerate(state):
        root = q / jnp.sqrt(bound)
        weights = product(product(vector, root), root)[0:1, :]
        mixing = weights * (127.0 ** -0.5) + infl[2 * mx + t] * root
        mixing = mixing - jnp.sum(mixing, axis=1, keepdims=True) * (1.0 / 128.0) + 1.0 / 128.0
        u_ref[2 * mx + t] = mixing
    pbuf[mx] = product(u_ref[2 * mx + 1], u_ref[2 * mx])
    pairs = [start(remote(pbuf.at[mx], pbuf.at[mx], at(mx + d, my))) for d in (1, 3, 2)]
    mine = u_ref.at[pl.ds(2 * mx, 2)]
    shared = [start(remote(mine, mine, at(mx + d, my))) for d in (1, 3, 2)]
    for copy in pairs:
        copy.wait_recv()

    p0, p1, p2, p3 = [pbuf[i] for i in range(4)]
    p23 = product(p3, p2)
    p03 = product(p23, product(p1, p0))
    vbuf[0] = p03
    rloc[0] = p03
    rloc[4] = p23
    rloc[6] = p3

    def applied(t):
        both = jnp.concatenate([u_ref[t], rloc[t]], axis=0)
        high, low = halves(both)
        out = jnp.dot(
            jnp.concatenate([high, low], axis=1), jnp.concatenate([xah[t], xah[t]], axis=0),
            preferred_element_type=F32,
        ) + jnp.dot(high, xal[t], preferred_element_type=F32)
        filter_ref[t] = out[0:128]
        yh, yl = halves(out[128:256])
        yloc[t, 0:128, :] = yh
        yloc[t, 128:256, :] = yl

    later = eye
    for level, d in enumerate((1, 2, 4, 8)):
        copy = remote(vbuf.at[level], vin.at[level], along(-d))

        @pl.when(tm >= d)
        def _(copy=copy):
            copy.start()

        if level == 0:
            for other_copy in shared:
                other_copy.wait_recv()
            r2 = product(p23, p1)
            rloc[2] = r2
            rloc[7] = u_ref[7]
            rloc[5] = product(p3, u_ref[5])
            rloc[3] = product(p23, u_ref[3])
            rloc[1] = product(r2, u_ref[1])
        applied(2 * level)
        applied(2 * level + 1)

        @pl.when(tm + d <= last_tm)
        def _(copy=copy):
            copy.wait_recv()

        @pl.when(tm + d > last_tm)
        def _(level=level):
            vin[level] = eye

        got = vin[level]
        if level < 3:
            vbuf[level + 1] = product(got, vbuf[level])
        later = product(got, later)

        @pl.when(tm >= d)
        def _(copy=copy):
            copy.wait_send()

    lh, ll = halves(later)
    wide = jnp.concatenate([lh, lh], axis=1)
    for t in range(8):
        smooth_ref[t] = jnp.dot(wide, yloc[t], preferred_element_type=F32) + jnp.dot(
            ll, yloc[t, 0:128, :], preferred_element_type=F32
        )
    for copy in sent:
        copy.wait_send()


def local(prior, observations, spread, inflation, tiles, targets):
    anywhere = pl.BlockSpec(memory_space=pl.ANY)
    vmem = pl.BlockSpec(memory_space=pltpu.VMEM)
    whole = jax.ShapeDtypeStruct(prior.shape, F32)
    return pl.pallas_call(
        assimilate,
        out_shape=(whole, whole),
        in_specs=[anywhere] * 6,
        out_specs=(vmem, vmem),
        scratch_shapes=[
            pltpu.VMEM((4, 4, 2, 128, 256), F32),
            pltpu.VMEM((4, 4096, 128), F32),
            pltpu.VMEM((2, 32, 256, 128), BF16),
            pltpu.VMEM((128, 256, 128), BF16),
            pltpu.VMEM((8, 128, 256), F32),
            pltpu.VMEM((8, 128, 256), BF16),
            pltpu.VMEM((8, 128, 256), BF16),
            pltpu.VMEM((4, 8, 512), F32),
            pltpu.VMEM((4, 4, 128), F32),
            pltpu.VMEM((4, 4, 8), jnp.int32),
            pltpu.SMEM((4, 4, 8), jnp.int32),
            pltpu.SMEM((8,), F32),
            pltpu.VMEM((2, 144, 256), F32),
            pltpu.VMEM((2, 136, 128), F32),
            pltpu.VMEM((4, 2, 136, 128), F32),
            pltpu.VMEM((8, 128, 128), F32),
            pltpu.VMEM((4, 128, 128), F32),
            pltpu.VMEM((4, 128, 128), F32),
            pltpu.VMEM((4, 128, 128), F32),
            pltpu.VMEM((8, 128, 128), F32),
            pltpu.VMEM((8, 256, 256), BF16),
            pltpu.SemaphoreType.DMA((96,)),
            pltpu.SemaphoreType.DMA((96,)),
            pltpu.SemaphoreType.DMA((8,)),
        ],
        compiler_params=pltpu.CompilerParams(
            collective_id=0, has_side_effects=True, vmem_limit_bytes=VMEM_LIMIT
        ),
        name="assimilate",
    )(prior, tiles.reshape(4096, 128), observations, spread.reshape(4, 128), targets, inflation)


def solution(mesh):
    placed = (
        P("tm", None, "row"),
        P("tm", "row"),
        P("row"),
        P("tm"),
        P("row", None, None, None),
        P("row", None),
    )
    return jax.shard_map(
        local,
        mesh=mesh,
        in_specs=placed,
        out_specs=(P("tm", None, "row"), P("tm", None, "row")),
        check_vma=False,
    )
```

time: 121 us -> 102 us (0.84)
  Pallas kernels: 113 us -> 97.4 us
  local copies, waits for them, and re-layouts: 7.14 us -> 3.33 us
    pallas_call x2 -> x1, Pallas kernels: 113 us -> 97.4 us  [local(): pl.pallas_call(assimilate, out_shape=(whole, whole), in_specs=[anywhere]...]
    unnamed x10 -> x4, local copies, waits for them, and re-layouts: 5.04 us -> 3.33 us
    pad x3 -> x0, local copies, waits for them, and re-layouts: 1.38 us -> none  [the longest x1 0.69 us: local(): spr = jnp.pad(spread.reshape(4, 128), ((0, 4), (0, 0)))]
where the time goes in v2:
time: 102 us; the launch traced here: 101 us
  Pallas kernels  97.4 us (95%)
  local copies, waits for them, and re-layouts  3.33 us (3%)
    pallas_call x1, Pallas kernels, local(): pl.pallas_call(assimilate, out_shape=(whole, whole), in_specs=[anywhere]...  97.4 us
    unnamed x4, local copies, waits for them, and re-layouts  3.33 us

profile of v2, /device:TPU:1, one launch (start us, length us, event | category | flops | bytes accessed | tf_op | source)
XLA Modules:
  0.0 101.3 jit_solution(9303551929144858617)
XLA Ops:
  0.6 97.4 %assimilate.1 = (f32[8,128,256]{2,1,0:T(8,128)}, f32[8,128,256]{2,1,0:T(8,128)}) custom-call(f32[8,128,256]{2,1,0:T(8,128)} %x_ref.1, f32[4096,128]{1,0:T(8,128)} %bitcast.2, f32[8,512]{1,0:T(8,128)} %obs_ref.1, f32[4,128]{1,0:T(4,128)} %bitcast.3, s32[4,8]{1,0:T(4,128)} %targets_ref.1, f32[8]{0:T(128)} %inflation_ref.1), custom_call_target="tpu_custom_call" | custom-call | tf_op jit(solution)/shard_map/assimilate/pallas_call | solution.py:380
  98.0 0.0 copy-start
  98.0 2.4 %copy.10 = f32[8,128,256]{2,1,0:T(8,128)} copy(f32[8,128,256]{2,1,0:T(8,128)} %get-tuple-element.4) | data formatting | bytes 2097152
  100.4 0.0 copy-done
  100.4 1.0 copy.11
Async XLA Ops:
  98.0 2.4 %copy-start = (f32[8,128,256]{2,1,0:T(8,128)S(1)}, f32[8,128,256]{2,1,0:T(8,128)}, u32[]{:S(2)}) copy-start(f32[8,128,256]{2,1,0:T(8,128)} %get-tuple-element.5) | copy-start | bytes 3145732

commit v3 on v2

--- a/solution.py
+++ b/solution.py
@@ -33,21 +33,23 @@
     return wide[:, :n] + wide[:, n:]
 
 
-PIECE = 192
+PIECE = 128
 SHARED = 16 * PIECE
 STEPS, BLOCK_ROWS = 2, 16
 
 
 def assimilate(
     x_ref, tiles_ref, obs_ref, spread_ref, targets_ref, inflation_ref,
-    smooth_ref, filter_ref,
+    filter_ref, y_ref, later_ref,
     xg, tg, xs, ts, xown, xah, xal, obg, spg, tgg, tgs, infl, acc, part, parts,
-    u_ref, pbuf, vbuf, vin, rloc, yloc,
-    send, recv, local_sem,
+    u_ref, pbuf, pown, pother, cown, cin, rloc, yloc, floc,
+    send, recv, local_sem, out_sem,
 ):
     tm, row = lax.axis_index("tm"), lax.axis_index("row")
     mx, my = lax.div(row, 4), lax.rem(row, 4)
-    last_tm = 15
+    core = lax.rem(tm, 2)
+    z = lax.div(tm, 2)
+    other = (tm + 1 - 2 * core, row)
     counter = [0]
 
     def at(x, y):
@@ -78,16 +80,18 @@
     for copy in own:
         copy.start()
 
+    eye = (
+        lax.broadcasted_iota(jnp.int32, (128, 128), 0) == lax.broadcasted_iota(jnp.int32, (128, 128), 1)
+    ).astype(F32)
+    for d in range(7):
+        cin[d] = eye
     barrier = pltpu.get_barrier_semaphore()
     near = [at(mx + d, my) for d in (1, 2, 3)] + [at(mx, my + d) for d in (1, 2, 3)]
-    near += [along(d) for d in (1, -1, 2, -2, 4, -4, 8)]
+    near += [other] + [along(2 * d) for d in range(1, 8)]
     for device in near:
         pl.semaphore_signal(barrier, inc=1, device_id=device, device_id_type=MESH)
     pl.semaphore_wait(barrier, len(near))
 
-    core = lax.rem(tm, 2)
-    z = lax.div(tm, 2)
-    other = (tm + 1 - 2 * core, row)
     sent = []
 
     def start(copy):
@@ -107,27 +111,23 @@
         up[t, k] = start(remote(src, xg.at[k, 1, t], at(mx, my + 1)))
         down[t, k] = start(remote(src, xg.at[k, 3, t], at(mx, my - 1)))
 
-    def send_y2(t):
-        up[t, 4] = start(remote(xg.at[:, 1, t, 0:64], xg.at[:, 2, t, 0:64], at(mx, my + 1)))
-        down[t, 4] = start(remote(xg.at[:, 3, t, 64:128], xg.at[:, 2, t, 64:128], at(mx, my - 1)))
+    far = {}
+
+    def pass_y(t, k):
+        up[t, k].wait_recv()
+        one = start(remote(xg.at[k, 1, t, 0:64], xg.at[k, 2, t, 0:64], at(mx, my + 1)))
+        down[t, k].wait_recv()
+        two = start(remote(xg.at[k, 3, t, 64:128], xg.at[k, 2, t, 64:128], at(mx, my - 1)))
+        far[t, k] = (one, two)
 
     send_across(0)
     send_y(0, 0)
+    send_y(1, 0)
     piece = pl.ds(PIECE * tm, PIECE)
     brought = [start(remote(tiles_ref.at[piece], tg.at[d, piece], at(mx + d, my))) for d in (1, 3, 2)]
-    send_across(1)
     rest = (4096 - SHARED) // 4
     first = pl.ds(SHARED + 2 * rest * core, rest)
     second = pl.ds(SHARED + 2 * rest * core + rest, rest)
-    right = [start(remote(tiles_ref.at[first], tg.at[1, first], at(mx + 1, my)))]
-    left = [start(remote(tiles_ref.at[second], tg.at[3, second], at(mx - 1, my)))]
-    right.append(start(remote(tiles_ref.at[second], tg.at[1, second], at(mx + 1, my))))
-    left.append(start(remote(tiles_ref.at[first], tg.at[3, first], at(mx - 1, my))))
-    small = []
-    for d in (1, 2, 3):
-        small.append(start(remote(obs_ref, obg.at[d], at(mx + d, my))))
-        small.append(start(remote(spread_ref, spg.at[d], at(mx + d, my))))
-        small.append(start(remote(targets_ref, tgg.at[d], at(mx + d, my))))
 
     passed = []
 
@@ -155,15 +155,15 @@
             xs[t, 2 * chunk + half, 0:128, :] = high
             xs[t, 2 * chunk + half, 128:256, :] = low
 
-    def split_tiles(k):
-        @pl.loop(0, 32)
+    def split_tiles(k, low, high_end):
+        @pl.loop(low, high_end)
         def _(n):
             high, low = halves(tg[k, pl.ds(pl.multiple_of(n * 128, 128), 128), :])
             ts[k * 32 + n, 0:128, :] = high
             ts[k * 32 + n, 128:256, :] = low
 
-    def observe(t, k):
-        for i in range(4):
+    def observe(t, k, rows=(0, 1, 2, 3)):
+        for i in rows:
             index = [tgs[k, i, j] for j in range(8)]
             state = jnp.concatenate([xs[t, j] for j in index], axis=1)
             block = jnp.concatenate([ts[(k * 4 + i) * 8 + j] for j in range(8)], axis=1)
@@ -190,37 +190,46 @@
 
     acc[...] = jnp.zeros_like(acc)
     chosen = [lax.broadcasted_iota(jnp.int32, (8, 128), 0) == 2 * mx + t for t in (0, 1)]
-    for d in (1, 3, 2):
-        across[0, d].wait_recv()
-        send_y(0, d)
+    across[0, 1].wait_recv()
+    send_y(0, 1)
+    across[0, 3].wait_recv()
+    send_y(0, 3)
+    send_across(1)
+    across[0, 2].wait_recv()
+    send_y(0, 2)
+    pass_y(0, 0)
+    pass_y(1, 0)
     for copy in brought:
         copy.wait_recv()
     steps = [send_z(1)]
     pass_on(unit(0))
-    send_y(1, 0)
+    right = [start(remote(tiles_ref.at[first], tg.at[1, first], at(mx + 1, my)))]
+    left = [start(remote(tiles_ref.at[second], tg.at[3, second], at(mx - 1, my)))]
+    small = []
+    for d in (1, 2, 3):
+        small.append(start(remote(obs_ref, obg.at[d], at(mx + d, my))))
+        small.append(start(remote(spread_ref, spg.at[d], at(mx + d, my))))
+        small.append(start(remote(targets_ref, tgg.at[d], at(mx + d, my))))
     for copy in own:
         copy.wait()
-    split_tiles(0)
+    split_tiles(0, 0, 32)
+    pass_y(0, 1)
+    pass_y(0, 3)
+    for d in (1, 3, 2):
+        across[1, d].wait_recv()
+        send_y(1, d)
+    right.append(start(remote(tiles_ref.at[second], tg.at[1, second], at(mx + 1, my))))
+    left.append(start(remote(tiles_ref.at[first], tg.at[3, first], at(mx - 1, my))))
+    pass_y(0, 2)
     for copy in steps[0]:
         copy.wait_recv()
     steps.append(send_z(2))
     pass_on(unit(-1))
     pass_on(unit(1))
-    for k in (0, 1, 3, 2):
-        up[0, k].wait_recv()
-        down[0, k].wait_recv()
-    send_y2(0)
-    for d in (1, 3, 2):
-        across[1, d].wait_recv()
-        send_y(1, d)
     right[0].wait_recv()
     right2 = start(remote(tg.at[1, first], tg.at[2, first], at(mx + 1, my)))
     left[0].wait_recv()
     left2 = start(remote(tg.at[3, second], tg.at[2, second], at(mx - 1, my)))
-    right[1].wait_recv()
-    left[1].wait_recv()
-    pass_on(tg.at[1, pl.ds(SHARED + 2 * rest * core, 2 * rest)])
-    pass_on(tg.at[3, pl.ds(SHARED + 2 * rest * core, 2 * rest)])
     for copy in small:
         copy.wait_recv()
     to_scalar = pltpu.make_async_copy(tgg, tgs, local_sem.at[0])
@@ -229,47 +238,61 @@
         split_state(0, k, 0)
         split_state(0, k, 1)
         split_state(0, k, 3)
+    pass_y(1, 1)
     for copy in steps[1]:
         copy.wait_recv()
     steps.append(send_z(3))
     pass_on(unit(-2))
     pass_on(unit(2))
-    for k in range(4):
+    for k in (0, 1, 3, 2):
+        for copy in far[0, k]:
+            copy.wait_recv()
+        split_state(0, k, 2)
         split_state(1, k, 0)
-    for t in range(8):
-        xah[t], xal[t] = halves(xown[t])
-    up[0, 4].wait_recv()
-    down[0, 4].wait_recv()
-    for k in range(4):
-        split_state(0, k, 2)
+    right[1].wait_recv()
+    pass_on(tg.at[1, pl.ds(SHARED + 2 * rest * core, 2 * rest)])
+    left[1].wait_recv()
+    pass_on(tg.at[3, pl.ds(SHARED + 2 * rest * core, 2 * rest)])
+    pass_y(1, 3)
     to_scalar.wait()
+    observe(0, 0, (0, 1))
+    pass_y(1, 2)
     for copy in steps[2]:
         copy.wait_recv()
     steps.append(send_z(4))
     pass_on(unit(-3))
     pass_on(unit(3))
-    observe(0, 0)
     right2.wait_recv()
     left2.wait_recv()
     pass_on(tg.at[2, pl.ds(SHARED + 2 * rest * core, 2 * rest)])
-    for k in (0, 1, 3, 2):
-        up[1, k].wait_recv()
-        down[1, k].wait_recv()
-    send_y2(1)
-    for copy in steps[3]:
-        copy.wait_recv()
-    pass_on(unit(4))
+    observe(0, 0, (2, 3))
+    for t in range(8):
+        xah[t], xal[t] = halves(xown[t])
     for k in range(4):
         split_state(1, k, 1)
         split_state(1, k, 3)
-    for copy in passed:
-        copy.wait_recv()
+    passed[5].wait_recv()
+    passed[6].wait_recv()
+    passed[9].wait_recv()
+    shared_tiles = SHARED // 128
+    for k in (1, 3):
+        split_tiles(k, shared_tiles, 32)
+        observe(0, k, (2, 3))
+    for copy in steps[3]:
+        copy.wait_recv()
+    pass_on(unit(4))
+    split_tiles(2, shared_tiles, 32)
+    observe(0, 2, (2, 3))
+    for i, copy in enumerate(passed):
+        if i not in (5, 6, 9):
+            copy.wait_recv()
     for k in (1, 2, 3):
-        split_tiles(k)
-        observe(0, k)
+        split_tiles(k, 0, shared_tiles)
+        observe(0, k, (0, 1))
     sums = reduce(0)
-    up[1, 4].wait_recv()
-    down[1, 4].wait_recv()
+    for k in (0, 1, 3, 2):
+        for copy in far[1, k]:
+            copy.wait_recv()
     for k in range(4):
         split_state(1, k, 2)
     for k in range(4):
@@ -278,9 +301,6 @@
     for copy in sums:
         copy.wait_recv()
 
-    eye = (
-        lax.broadcasted_iota(jnp.int32, (128, 128), 0) == lax.broadcasted_iota(jnp.int32, (128, 128), 1)
-    ).astype(F32)
     state = []
     for t in (0, 1):
         total = part[t] + parts[1, t] + parts[2, t] + parts[3, t]
@@ -309,79 +329,104 @@
     p0, p1, p2, p3 = [pbuf[i] for i in range(4)]
     p23 = product(p3, p2)
     p03 = product(p23, product(p1, p0))
-    vbuf[0] = p03
+    pown[...] = p03
+    swap = start(remote(pown, pother, other))
     rloc[0] = p03
     rloc[4] = p23
     rloc[6] = p3
-
-    def applied(t):
+    swap.wait_recv()
+    theirs = pother[...]
+    odd = core == 1
+    cown[...] = product(jnp.where(odd, p03, theirs), jnp.where(odd, theirs, p03))
+    half_rows = pl.ds(64 * core, 64)
+    down_z = []
+    for d in range(1, 8):
+        copy = remote(cown.at[half_rows], cin.at[d - 1, half_rows], along(-2 * d))
+        down_z.append(copy)
+
+        @pl.when(z >= d)
+        def _(copy=copy):
+            copy.start()
+
+    for copy in shared:
+        copy.wait_recv()
+    r2 = product(p23, p1)
+    rloc[2] = r2
+    rloc[7] = u_ref[7]
+    rloc[5] = product(p3, u_ref[5])
+    rloc[3] = product(p23, u_ref[3])
+    rloc[1] = product(r2, u_ref[1])
+    stored = []
+    for t in range(8):
         both = jnp.concatenate([u_ref[t], rloc[t]], axis=0)
         high, low = halves(both)
         out = jnp.dot(
             jnp.concatenate([high, low], axis=1), jnp.concatenate([xah[t], xah[t]], axis=0),
             preferred_element_type=F32,
         ) + jnp.dot(high, xal[t], preferred_element_type=F32)
-        filter_ref[t] = out[0:128]
+        floc[t] = out[0:128]
         yh, yl = halves(out[128:256])
         yloc[t, 0:128, :] = yh
         yloc[t, 128:256, :] = yl
-
-    later = eye
-    for level, d in enumerate((1, 2, 4, 8)):
-        copy = remote(vbuf.at[level], vin.at[level], along(-d))
-
-        @pl.when(tm >= d)
-        def _(copy=copy):
-            copy.start()
-
-        if level == 0:
-            for other_copy in shared:
-                other_copy.wait_recv()
-            r2 = product(p23, p1)
-            rloc[2] = r2
-            rloc[7] = u_ref[7]
-            rloc[5] = product(p3, u_ref[5])
-            rloc[3] = product(p23, u_ref[3])
-            rloc[1] = product(r2, u_ref[1])
-        applied(2 * level)
-        applied(2 * level + 1)
-
-        @pl.when(tm + d <= last_tm)
-        def _(copy=copy):
+        for i, (src, dst) in enumerate(((floc, filter_ref), (yloc, y_ref))):
+            stored.append(pltpu.make_async_copy(src.at[t], dst.at[t], out_sem.at[i, t]))
+            stored[-1].start()
+
+    for d in range(1, 8):
+        @pl.when(z + d <= 7)
+        def _(copy=down_z[d - 1]):
             copy.wait_recv()
 
-        @pl.when(tm + d > last_tm)
-        def _(level=level):
-            vin[level] = eye
-
-        got = vin[level]
-        if level < 3:
-            vbuf[level + 1] = product(got, vbuf[level])
-        later = product(got, later)
-
-        @pl.when(tm >= d)
-        def _(copy=copy):
+    halves_swap = start(remote(cin.at[:, half_rows], cin.at[:, half_rows], other))
+    halves_swap.wait_recv()
+    c = [cin[d] for d in range(7)]
+    upper = product(product(c[6], c[5]), product(c[4], c[3]))
+    later = product(upper, product(product(c[2], c[1]), c[0]))
+    later_ref[...] = jnp.where(odd, later, product(later, theirs))
+    for copy in stored:
+        copy.wait()
+    for d in range(1, 8):
+        @pl.when(z >= d)
+        def _(copy=down_z[d - 1]):
             copy.wait_send()
 
-    lh, ll = halves(later)
-    wide = jnp.concatenate([lh, lh], axis=1)
-    for t in range(8):
-        smooth_ref[t] = jnp.dot(wide, yloc[t], preferred_element_type=F32) + jnp.dot(
-            ll, yloc[t, 0:128, :], preferred_element_type=F32
-        )
     for copy in sent:
         copy.wait_send()
+
+
+def smooth(later_ref, y_hbm, filter_hbm, smooth_out, filter_out, y, f, out, sem):
+    f_in = pltpu.make_async_copy(filter_hbm, f, sem.at[16])
+    f_out = pltpu.make_async_copy(f, filter_out, sem.at[17])
+    y_in = [pltpu.make_async_copy(y_hbm.at[t], y.at[t], sem.at[t]) for t in range(8)]
+    out_t = [pltpu.make_async_copy(out.at[t], smooth_out.at[t], sem.at[8 + t]) for t in range(8)]
+    for copy in y_in:
+        copy.start()
+    f_in.start()
+    high, low = halves(later_ref[...])
+    wide = jnp.concatenate([high, high], axis=1)
+    for t in range(8):
+        y_in[t].wait()
+        out[t] = jnp.dot(wide, y[t], preferred_element_type=F32) + jnp.dot(
+            low, y[t, 0:128, :], preferred_element_type=F32
+        )
+        out_t[t].start()
+        if t == 3:
+            f_in.wait()
+            f_out.start()
+    f_out.wait()
+    for copy in out_t:
+        copy.wait()
 
 
 def local(prior, observations, spread, inflation, tiles, targets):
     anywhere = pl.BlockSpec(memory_space=pl.ANY)
     vmem = pl.BlockSpec(memory_space=pltpu.VMEM)
     whole = jax.ShapeDtypeStruct(prior.shape, F32)
-    return pl.pallas_call(
+    filtered, y, later = pl.pallas_call(
         assimilate,
-        out_shape=(whole, whole),
+        out_shape=(whole, jax.ShapeDtypeStruct((8, 256, 256), BF16), jax.ShapeDtypeStruct((128, 128), F32)),
         in_specs=[anywhere] * 6,
-        out_specs=(vmem, vmem),
+        out_specs=(anywhere, anywhere, vmem),
         scratch_shapes=[
             pltpu.VMEM((4, 4, 2, 128, 256), F32),
             pltpu.VMEM((4, 4096, 128), F32),
@@ -400,19 +445,37 @@
             pltpu.VMEM((4, 2, 136, 128), F32),
             pltpu.VMEM((8, 128, 128), F32),
             pltpu.VMEM((4, 128, 128), F32),
-            pltpu.VMEM((4, 128, 128), F32),
-            pltpu.VMEM((4, 128, 128), F32),
+            pltpu.VMEM((128, 128), F32),
+            pltpu.VMEM((128, 128), F32),
+            pltpu.VMEM((128, 128), F32),
+            pltpu.VMEM((7, 128, 128), F32),
             pltpu.VMEM((8, 128, 128), F32),
             pltpu.VMEM((8, 256, 256), BF16),
-            pltpu.SemaphoreType.DMA((96,)),
-            pltpu.SemaphoreType.DMA((96,)),
+            pltpu.VMEM((8, 128, 256), F32),
+            pltpu.SemaphoreType.DMA((112,)),
+            pltpu.SemaphoreType.DMA((112,)),
             pltpu.SemaphoreType.DMA((8,)),
+            pltpu.SemaphoreType.DMA((2, 8)),
         ],
         compiler_params=pltpu.CompilerParams(
             collective_id=0, has_side_effects=True, vmem_limit_bytes=VMEM_LIMIT
         ),
         name="assimilate",
     )(prior, tiles.reshape(4096, 128), observations, spread.reshape(4, 128), targets, inflation)
+    return pl.pallas_call(
+        smooth,
+        out_shape=(whole, whole),
+        in_specs=[vmem, anywhere, anywhere],
+        out_specs=(anywhere, anywhere),
+        scratch_shapes=[
+            pltpu.VMEM((8, 256, 256), BF16),
+            pltpu.VMEM((8, 128, 256), F32),
+            pltpu.VMEM((8, 128, 256), F32),
+            pltpu.SemaphoreType.DMA((18,)),
+        ],
+        compiler_params=pltpu.CompilerParams(vmem_limit_bytes=VMEM_LIMIT),
+        name="smooth",
+    )(later, y, filtered)
 
 
 def solution(mesh):

time: 102 us -> 93.6 us (0.918)
  Pallas kernels: 97.4 us -> 92.9 us
  local copies, waits for them, and re-layouts: 3.33 us -> 0 us
    pallas_call x1 -> x2, Pallas kernels: 97.4 us -> 92.9 us  [the longest x1 88.7 us: local(): pl.pallas_call(assimilate, out_shape=(whole, jax.ShapeDtypeStruct((8, 256...]
    unnamed x4 -> x0, local copies, waits for them, and re-layouts: 3.33 us -> none
where the time goes in v3:
time: 93.6 us; the launch traced here: 93.5 us
  Pallas kernels  92.9 us (99%)
    pallas_call x1, Pallas kernels, local(): pl.pallas_call(assimilate, out_shape=(whole, jax.ShapeDtypeStruct((8, 256...  88.7 us
    pallas_call x1, Pallas kernels, local(): pl.pallas_call(smooth, out_shape=(whole, whole), in_specs=[vmem, anywhere...  4.17 us

profile of v3, /device:TPU:1, one launch (start us, length us, event | category | flops | bytes accessed | tf_op | source)
XLA Modules:
  0.0 93.5 jit_solution(3991672881005579729)
XLA Ops:
  0.6 88.7 %assimilate.1 = (f32[8,128,256]{2,1,0:T(8,128)}, bf16[8,256,256]{2,1,0:T(8,128)(2,1)}, f32[128,128]{1,0:T(8,128)}) custom-call(f32[8,128,256]{2,1,0:T(8,128)} %x_ref.1, f32[4096,128]{1,0:T(8,128)} %bitcast.2, f32[8,512]{1,0:T(8,128)} %obs_ref.1, f32[4,128]{1,0:T(4,128)} %bitcast.3, s32[4,8]{1,0:T(4,128)} %targets_ref.1, f32[8]{0:T(128)} %inflation_ref.1), custom_call_target="tpu_custom_call" | custom-call | tf_op jit(solution)/shard_map/assimilate/pallas_call | solution.py:425
  89.3 4.2 %smooth.1 = (f32[8,128,256]{2,1,0:T(8,128)}, f32[8,128,256]{2,1,0:T(8,128)}) custom-call(f32[128,128]{1,0:T(8,128)} %get-tuple-element.5.later_ref, bf16[8,256,256]{2,1,0:T(8,128)(2,1)} %get-tuple-element.6.y_hbm, f32[8,128,256]{2,1,0:T(8,128)} %get-tuple-element.7.filter_hbm), custom_call_target="tpu_custom_call" | custom-call | tf_op jit(solution)/shard_map/smooth/pallas_call | solution.py:465

commit v4 on v3

--- a/solution.py
+++ b/solution.py
@@ -9,7 +9,7 @@
 
 MESH = pl.DeviceIdType.MESH
 NS_ITERS = 8
-VMEM_LIMIT = 58 << 20
+VMEM_LIMIT = 40 << 20
 F32, BF16 = jnp.float32, jnp.bfloat16
 NT = (((1,), (1,)), ((), ()))
 
@@ -42,8 +42,8 @@
     x_ref, tiles_ref, obs_ref, spread_ref, targets_ref, inflation_ref,
     filter_ref, y_ref, later_ref,
     xg, tg, xs, ts, xown, xah, xal, obg, spg, tgg, tgs, infl, acc, part, parts,
-    u_ref, pbuf, pown, pother, cown, cin, rloc, yloc, floc,
-    send, recv, local_sem, out_sem,
+    u_ref, pbuf, pown, pother, cown, cin, rloc,
+    send, recv, local_sem,
 ):
     tm, row = lax.axis_index("tm"), lax.axis_index("row")
     mx, my = lax.div(row, 4), lax.rem(row, 4)
@@ -321,10 +321,10 @@
         u_ref[2 * mx + t] = mixing
     pbuf[mx] = product(u_ref[2 * mx + 1], u_ref[2 * mx])
     pairs = [start(remote(pbuf.at[mx], pbuf.at[mx], at(mx + d, my))) for d in (1, 3, 2)]
+    for copy in pairs:
+        copy.wait_recv()
     mine = u_ref.at[pl.ds(2 * mx, 2)]
     shared = [start(remote(mine, mine, at(mx + d, my))) for d in (1, 3, 2)]
-    for copy in pairs:
-        copy.wait_recv()
 
     p0, p1, p2, p3 = [pbuf[i] for i in range(4)]
     p23 = product(p3, p2)
@@ -339,10 +339,10 @@
     odd = core == 1
     cown[...] = product(jnp.where(odd, p03, theirs), jnp.where(odd, theirs, p03))
     half_rows = pl.ds(64 * core, 64)
-    down_z = []
-    for d in range(1, 8):
+    down_z = {}
+    for d in (4, 3, 5, 2, 6, 1, 7):
         copy = remote(cown.at[half_rows], cin.at[d - 1, half_rows], along(-2 * d))
-        down_z.append(copy)
+        down_z[d] = copy
 
         @pl.when(z >= d)
         def _(copy=copy):
@@ -356,7 +356,6 @@
     rloc[5] = product(p3, u_ref[5])
     rloc[3] = product(p23, u_ref[3])
     rloc[1] = product(r2, u_ref[1])
-    stored = []
     for t in range(8):
         both = jnp.concatenate([u_ref[t], rloc[t]], axis=0)
         high, low = halves(both)
@@ -364,17 +363,14 @@
             jnp.concatenate([high, low], axis=1), jnp.concatenate([xah[t], xah[t]], axis=0),
             preferred_element_type=F32,
         ) + jnp.dot(high, xal[t], preferred_element_type=F32)
-        floc[t] = out[0:128]
+        filter_ref[t] = out[0:128]
         yh, yl = halves(out[128:256])
-        yloc[t, 0:128, :] = yh
-        yloc[t, 128:256, :] = yl
-        for i, (src, dst) in enumerate(((floc, filter_ref), (yloc, y_ref))):
-            stored.append(pltpu.make_async_copy(src.at[t], dst.at[t], out_sem.at[i, t]))
-            stored[-1].start()
+        y_ref[t, 0:128, :] = yh
+        y_ref[t, 128:256, :] = yl
 
     for d in range(1, 8):
         @pl.when(z + d <= 7)
-        def _(copy=down_z[d - 1]):
+        def _(copy=down_z[d]):
             copy.wait_recv()
 
     halves_swap = start(remote(cin.at[:, half_rows], cin.at[:, half_rows], other))
@@ -383,36 +379,26 @@
     upper = product(product(c[6], c[5]), product(c[4], c[3]))
     later = product(upper, product(product(c[2], c[1]), c[0]))
     later_ref[...] = jnp.where(odd, later, product(later, theirs))
-    for copy in stored:
-        copy.wait()
     for d in range(1, 8):
         @pl.when(z >= d)
-        def _(copy=down_z[d - 1]):
+        def _(copy=down_z[d]):
             copy.wait_send()
 
     for copy in sent:
         copy.wait_send()
 
 
-def smooth(later_ref, y_hbm, filter_hbm, smooth_out, filter_out, y, f, out, sem):
-    f_in = pltpu.make_async_copy(filter_hbm, f, sem.at[16])
-    f_out = pltpu.make_async_copy(f, filter_out, sem.at[17])
-    y_in = [pltpu.make_async_copy(y_hbm.at[t], y.at[t], sem.at[t]) for t in range(8)]
-    out_t = [pltpu.make_async_copy(out.at[t], smooth_out.at[t], sem.at[8 + t]) for t in range(8)]
-    for copy in y_in:
-        copy.start()
-    f_in.start()
+def smooth(later_ref, y_ref, filter_ref, smooth_out, filter_out, out, sem):
+    f_out = pltpu.make_async_copy(filter_ref, filter_out, sem.at[8])
+    out_t = [pltpu.make_async_copy(out.at[t], smooth_out.at[t], sem.at[t]) for t in range(8)]
+    f_out.start()
     high, low = halves(later_ref[...])
     wide = jnp.concatenate([high, high], axis=1)
     for t in range(8):
-        y_in[t].wait()
-        out[t] = jnp.dot(wide, y[t], preferred_element_type=F32) + jnp.dot(
-            low, y[t, 0:128, :], preferred_element_type=F32
+        out[t] = jnp.dot(wide, y_ref[t], preferred_element_type=F32) + jnp.dot(
+            low, y_ref[t, 0:128, :], preferred_element_type=F32
         )
         out_t[t].start()
-        if t == 3:
-            f_in.wait()
-            f_out.start()
     f_out.wait()
     for copy in out_t:
         copy.wait()
@@ -426,7 +412,7 @@
         assimilate,
         out_shape=(whole, jax.ShapeDtypeStruct((8, 256, 256), BF16), jax.ShapeDtypeStruct((128, 128), F32)),
         in_specs=[anywhere] * 6,
-        out_specs=(anywhere, anywhere, vmem),
+        out_specs=(vmem, vmem, vmem),
         scratch_shapes=[
             pltpu.VMEM((4, 4, 2, 128, 256), F32),
             pltpu.VMEM((4, 4096, 128), F32),
@@ -450,30 +436,28 @@
             pltpu.VMEM((128, 128), F32),
             pltpu.VMEM((7, 128, 128), F32),
             pltpu.VMEM((8, 128, 128), F32),
-            pltpu.VMEM((8, 256, 256), BF16),
-            pltpu.VMEM((8, 128, 256), F32),
             pltpu.SemaphoreType.DMA((112,)),
             pltpu.SemaphoreType.DMA((112,)),
             pltpu.SemaphoreType.DMA((8,)),
-            pltpu.SemaphoreType.DMA((2, 8)),
         ],
         compiler_params=pltpu.CompilerParams(
             collective_id=0, has_side_effects=True, vmem_limit_bytes=VMEM_LIMIT
         ),
         name="assimilate",
-    )(prior, tiles.reshape(4096, 128), observations, spread.reshape(4, 128), targets, inflation)
+    )(*[
+        pltpu.with_memory_space_constraint(array, pltpu.HBM)
+        for array in (prior, tiles.reshape(4096, 128), observations, spread.reshape(4, 128), targets, inflation)
+    ])
     return pl.pallas_call(
         smooth,
         out_shape=(whole, whole),
-        in_specs=[vmem, anywhere, anywhere],
+        in_specs=[vmem, vmem, vmem],
         out_specs=(anywhere, anywhere),
         scratch_shapes=[
-            pltpu.VMEM((8, 256, 256), BF16),
             pltpu.VMEM((8, 128, 256), F32),
-            pltpu.VMEM((8, 128, 256), F32),
-            pltpu.SemaphoreType.DMA((18,)),
+            pltpu.SemaphoreType.DMA((9,)),
         ],
-        compiler_params=pltpu.CompilerParams(vmem_limit_bytes=VMEM_LIMIT),
+        compiler_params=pltpu.CompilerParams(vmem_limit_bytes=16 << 20),
         name="smooth",
     )(later, y, filtered)
 

time: 93.6 us -> 89.4 us (0.955)
  Pallas kernels: 92.9 us -> 88.7 us
    pallas_call x1, Pallas kernels: 4.17 us -> 1.38 us  [local(): pl.pallas_call(smooth, out_shape=(whole, whole), in_specs=[vmem, vmem, vm...]
    pallas_call x1, Pallas kernels: 88.7 us -> 87.3 us  [local(): pl.pallas_call(assimilate, out_shape=(whole, jax.ShapeDtypeStruct((8, 256...]
where the time goes in v4:
time: 89.4 us
  Pallas kernels  88.7 us (99%)
    pallas_call x1, Pallas kernels, local(): pl.pallas_call(assimilate, out_shape=(whole, jax.ShapeDtypeStruct((8, 256...  87.3 us

profile of v4, /device:TPU:1, one launch (start us, length us, event | category | flops | bytes accessed | tf_op | source)
XLA Modules:
  0.0 89.4 jit_solution(11739409768404406517)
XLA Ops:
  0.6 87.3 %assimilate.1 = (f32[8,128,256]{2,1,0:T(8,128)S(1)}, bf16[8,256,256]{2,1,0:T(8,128)(2,1)S(1)}, f32[128,128]{1,0:T(8,128)S(1)}) custom-call(f32[8,128,256]{2,1,0:T(8,128)} %x_ref.1, f32[4096,128]{1,0:T(8,128)} %bitcast.2, f32[8,512]{1,0:T(8,128)} %obs_ref.1, f32[4,128]{1,0:T(4,128)} %bitcast.3, s32[4,8]{1,0:T(4,128)} %targets_ref.1, f32[8]{0:T(128)} %inflation_ref.1), custom_call_target="tpu_custom_call" | custom-call | tf_op jit(solution)/shard_map/assimilate/pallas_call | solution.py:411
  88.0 1.4 %smooth.1 = (f32[8,128,256]{2,1,0:T(8,128)}, f32[8,128,256]{2,1,0:T(8,128)}) custom-call(f32[128,128]{1,0:T(8,128)S(1)} %get-tuple-element.5.later_ref, bf16[8,256,256]{2,1,0:T(8,128)(2,1)S(1)} %get-tuple-element.6.y_ref, f32[8,128,256]{2,1,0:T(8,128)S(1)} %get-tuple-element.7.filter_ref), custom_call_target="tpu_custom_call" | custom-call | tf_op jit(solution)/shard_map/smooth/pallas_call | solution.py:451

commit v5 on v4

--- a/solution.py
+++ b/solution.py
@@ -129,6 +129,7 @@
     first = pl.ds(SHARED + 2 * rest * core, rest)
     second = pl.ds(SHARED + 2 * rest * core + rest, rest)
 
+    send_across(1)
     passed = []
 
     def unit(step, low=0, size=PIECE):
@@ -163,6 +164,7 @@
             ts[k * 32 + n, 128:256, :] = low
 
     def observe(t, k, rows=(0, 1, 2, 3)):
+        lefts, rights = [], []
         for i in rows:
             index = [tgs[k, i, j] for j in range(8)]
             state = jnp.concatenate([xs[t, j] for j in index], axis=1)
@@ -177,10 +179,11 @@
             ih, il = halves(jnp.broadcast_to(innovation, (16, 128)))
             upper = lax.broadcasted_iota(jnp.int32, (16, 128), 0) < 8
             lines = jnp.where(upper, ih.astype(F32), il.astype(F32)).astype(BF16)
-            acc[t] += lax.dot_general(
-                jnp.concatenate([wh, lines], axis=0), jnp.concatenate([wh, wl], axis=0), NT,
-                preferred_element_type=F32,
-            )
+            lefts.append(jnp.concatenate([wh, lines], axis=0))
+            rights.append(jnp.concatenate([wh, wl], axis=0))
+        acc[t] += lax.dot_general(
+            jnp.concatenate(lefts, axis=1), jnp.concatenate(rights, axis=1), NT, preferred_element_type=F32
+        )
 
     def reduce(t):
         cross = acc[t, 0:128, 128:256]
@@ -194,17 +197,16 @@
     send_y(0, 1)
     across[0, 3].wait_recv()
     send_y(0, 3)
-    send_across(1)
     across[0, 2].wait_recv()
     send_y(0, 2)
+    right = [start(remote(tiles_ref.at[first], tg.at[1, first], at(mx + 1, my)))]
+    left = [start(remote(tiles_ref.at[second], tg.at[3, second], at(mx - 1, my)))]
     pass_y(0, 0)
     pass_y(1, 0)
     for copy in brought:
         copy.wait_recv()
     steps = [send_z(1)]
     pass_on(unit(0))
-    right = [start(remote(tiles_ref.at[first], tg.at[1, first], at(mx + 1, my)))]
-    left = [start(remote(tiles_ref.at[second], tg.at[3, second], at(mx - 1, my)))]
     small = []
     for d in (1, 2, 3):
         small.append(start(remote(obs_ref, obg.at[d], at(mx + d, my))))
@@ -215,17 +217,17 @@
     split_tiles(0, 0, 32)
     pass_y(0, 1)
     pass_y(0, 3)
+    for copy in steps[0]:
+        copy.wait_recv()
+    steps.append(send_z(2))
+    pass_on(unit(-1))
+    pass_on(unit(1))
     for d in (1, 3, 2):
         across[1, d].wait_recv()
         send_y(1, d)
     right.append(start(remote(tiles_ref.at[second], tg.at[1, second], at(mx + 1, my))))
     left.append(start(remote(tiles_ref.at[first], tg.at[3, first], at(mx - 1, my))))
     pass_y(0, 2)
-    for copy in steps[0]:
-        copy.wait_recv()
-    steps.append(send_z(2))
-    pass_on(unit(-1))
-    pass_on(unit(1))
     right[0].wait_recv()
     right2 = start(remote(tg.at[1, first], tg.at[2, first], at(mx + 1, my)))
     left[0].wait_recv()
@@ -275,20 +277,21 @@
     passed[6].wait_recv()
     passed[9].wait_recv()
     shared_tiles = SHARED // 128
+    shared_rows, direct_rows = range(SHARED // 1024), range(SHARED // 1024, 4)
     for k in (1, 3):
         split_tiles(k, shared_tiles, 32)
-        observe(0, k, (2, 3))
+        observe(0, k, direct_rows)
     for copy in steps[3]:
         copy.wait_recv()
     pass_on(unit(4))
     split_tiles(2, shared_tiles, 32)
-    observe(0, 2, (2, 3))
+    observe(0, 2, direct_rows)
     for i, copy in enumerate(passed):
         if i not in (5, 6, 9):
             copy.wait_recv()
     for k in (1, 2, 3):
         split_tiles(k, 0, shared_tiles)
-        observe(0, k, (0, 1))
+        observe(0, k, shared_rows)
     sums = reduce(0)
     for k in (0, 1, 3, 2):
         for copy in far[1, k]:
@@ -368,6 +371,9 @@
         y_ref[t, 0:128, :] = yh
         y_ref[t, 128:256, :] = yl
 
+    for copy in sent:
+        copy.wait_send()
+    sent.clear()
     for d in range(1, 8):
         @pl.when(z + d <= 7)
         def _(copy=down_z[d]):

time: 89.4 us -> 86.9 us (0.972)
  Pallas kernels: 88.7 us -> 86.2 us
    pallas_call x1, Pallas kernels: 87.3 us -> 84.8 us  [local(): pl.pallas_call(assimilate, out_shape=(whole, jax.ShapeDtypeStruct((8, 256...]
where the time goes in v5:
time: 86.9 us; the launch traced here: 86.8 us
  Pallas kernels  86.2 us (99%)
    pallas_call x1, Pallas kernels, local(): pl.pallas_call(assimilate, out_shape=(whole, jax.ShapeDtypeStruct((8, 256...  84.8 us

profile of v5, /device:TPU:1, one launch (start us, length us, event | category | flops | bytes accessed | tf_op | source)
XLA Modules:
  0.0 86.8 jit_solution(6006204481682660595)
XLA Ops:
  0.6 84.8 %assimilate.1 = (f32[8,128,256]{2,1,0:T(8,128)S(1)}, bf16[8,256,256]{2,1,0:T(8,128)(2,1)S(1)}, f32[128,128]{1,0:T(8,128)S(1)}) custom-call(f32[8,128,256]{2,1,0:T(8,128)} %x_ref.1, f32[4096,128]{1,0:T(8,128)} %bitcast.2, f32[8,512]{1,0:T(8,128)} %obs_ref.1, f32[4,128]{1,0:T(4,128)} %bitcast.3, s32[4,8]{1,0:T(4,128)} %targets_ref.1, f32[8]{0:T(128)} %inflation_ref.1), custom_call_target="tpu_custom_call" | custom-call | tf_op jit(solution)/shard_map/assimilate/pallas_call | solution.py:417
  85.4 1.4 %smooth.1 = (f32[8,128,256]{2,1,0:T(8,128)}, f32[8,128,256]{2,1,0:T(8,128)}) custom-call(f32[128,128]{1,0:T(8,128)S(1)} %get-tuple-element.5.later_ref, bf16[8,256,256]{2,1,0:T(8,128)(2,1)S(1)} %get-tuple-element.6.y_ref, f32[8,128,256]{2,1,0:T(8,128)S(1)} %get-tuple-element.7.filter_ref), custom_call_target="tpu_custom_call" | custom-call | tf_op jit(solution)/shard_map/smooth/pallas_call | solution.py:457

commit v6 on v5

--- a/solution.py
+++ b/solution.py
@@ -163,9 +163,9 @@
             ts[k * 32 + n, 0:128, :] = high
             ts[k * 32 + n, 128:256, :] = low
 
-    def observe(t, k, rows=(0, 1, 2, 3)):
+    def observe(t, blocks, rows=(0, 1, 2, 3)):
         lefts, rights = [], []
-        for i in rows:
+        for k, i in [(k, i) for k in blocks for i in rows]:
             index = [tgs[k, i, j] for j in range(8)]
             state = jnp.concatenate([xs[t, j] for j in index], axis=1)
             block = jnp.concatenate([ts[(k * 4 + i) * 8 + j] for j in range(8)], axis=1)
@@ -257,7 +257,7 @@
     pass_on(tg.at[3, pl.ds(SHARED + 2 * rest * core, 2 * rest)])
     pass_y(1, 3)
     to_scalar.wait()
-    observe(0, 0, (0, 1))
+    observe(0, (0,), (0, 1))
     pass_y(1, 2)
     for copy in steps[2]:
         copy.wait_recv()
@@ -267,7 +267,7 @@
     right2.wait_recv()
     left2.wait_recv()
     pass_on(tg.at[2, pl.ds(SHARED + 2 * rest * core, 2 * rest)])
-    observe(0, 0, (2, 3))
+    observe(0, (0,), (2, 3))
     for t in range(8):
         xah[t], xal[t] = halves(xown[t])
     for k in range(4):
@@ -280,26 +280,25 @@
     shared_rows, direct_rows = range(SHARED // 1024), range(SHARED // 1024, 4)
     for k in (1, 3):
         split_tiles(k, shared_tiles, 32)
-        observe(0, k, direct_rows)
+        observe(0, (k,), direct_rows)
     for copy in steps[3]:
         copy.wait_recv()
     pass_on(unit(4))
     split_tiles(2, shared_tiles, 32)
-    observe(0, 2, direct_rows)
+    observe(0, (2,), direct_rows)
     for i, copy in enumerate(passed):
         if i not in (5, 6, 9):
             copy.wait_recv()
     for k in (1, 2, 3):
         split_tiles(k, 0, shared_tiles)
-        observe(0, k, shared_rows)
+    observe(0, (1, 2, 3), shared_rows)
     sums = reduce(0)
     for k in (0, 1, 3, 2):
         for copy in far[1, k]:
             copy.wait_recv()
     for k in range(4):
         split_state(1, k, 2)
-    for k in range(4):
-        observe(1, k)
+    observe(1, range(4))
     sums += reduce(1)
     for copy in sums:
         copy.wait_recv()

time: 86.9 us -> 86.7 us (level)
  no operation moved by 1% of the time
where the time goes in v6:
time: 86.7 us; the launch traced here: 86.6 us
  Pallas kernels  86 us (99%)
    pallas_call x1, Pallas kernels, local(): pl.pallas_call(assimilate, out_shape=(whole, jax.ShapeDtypeStruct((8, 256...  84.6 us

profile of v6, /device:TPU:1, one launch (start us, length us, event | category | flops | bytes accessed | tf_op | source)
XLA Modules:
  0.0 86.6 jit_solution(14165270359147133766)
XLA Ops:
  0.6 84.6 %assimilate.1 = (f32[8,128,256]{2,1,0:T(8,128)S(1)}, bf16[8,256,256]{2,1,0:T(8,128)(2,1)S(1)}, f32[128,128]{1,0:T(8,128)S(1)}) custom-call(f32[8,128,256]{2,1,0:T(8,128)} %x_ref.1, f32[4096,128]{1,0:T(8,128)} %bitcast.2, f32[8,512]{1,0:T(8,128)} %obs_ref.1, f32[4,128]{1,0:T(4,128)} %bitcast.3, s32[4,8]{1,0:T(4,128)} %targets_ref.1, f32[8]{0:T(128)} %inflation_ref.1), custom_call_target="tpu_custom_call" | custom-call | tf_op jit(solution)/shard_map/assimilate/pallas_call | solution.py:416
  85.2 1.4 %smooth.1 = (f32[8,128,256]{2,1,0:T(8,128)}, f32[8,128,256]{2,1,0:T(8,128)}) custom-call(f32[128,128]{1,0:T(8,128)S(1)} %get-tuple-element.5.later_ref, bf16[8,256,256]{2,1,0:T(8,128)(2,1)S(1)} %get-tuple-element.6.y_ref, f32[8,128,256]{2,1,0:T(8,128)S(1)} %get-tuple-element.7.filter_ref), custom_call_target="tpu_custom_call" | custom-call | tf_op jit(solution)/shard_map/smooth/pallas_call | solution.py:456
